TPU v7x, 32 devices: a whole 2x2x4 slice. The times are simulated.
32 devices in a mesh: slab: 4 (over y, x), brick: 8 (over z, core).
Axes of the slice: x: 2, y: 2, z: 4, core: 2. Of those that a mesh axis runs over, the one named last changes fastest.
Arguments:
- k_coeffs: float32 [8, 16, 16, 128], P('slab', 'brick'), may hold values from -0.3 to 0.4
- v_basis: float32 [32768, 128], P(('slab', 'brick')), may hold values from -4 to 4
Outputs:
- basis_x: float32 [8, 16, 16, 128], P('slab', 'brick')
- coupling: float32 [128, 128], replicated
- basis_v: float32 [32768, 128], P(('slab', 'brick'))
All inputs are finite; a program needn't handle non-finite values.
Results may differ from a plain program's by a relative error of at most 0.0001.
Values sent between devices are 32-bit elements; how exact they have to be, the bound alone decides.
A program may use at most 64 MiB of HBM per device.

v0:
```python
import functools
import math

import jax
import jax.numpy as jnp
from jax import lax
from jax.experimental import pallas as pl
from jax.experimental.pallas import tpu as pltpu
from jax.sharding import PartitionSpec as P

NVX = 32

CFL = 0.9
VMAX = 6.0
COLLIDE = 0.3
RHO_MIN = 0.25
TEMP_MIN = 0.25
PRECISE = lax.Precision.HIGHEST
FAST = lax.Precision.HIGH
MESH = pl.DeviceIdType.MESH
VM = pl.BlockSpec(memory_space=pltpu.VMEM)


def dims():
    return 2, lax.axis_size("slab"), lax.axis_size("brick") // 2


def place():
    brick = lax.axis_index("brick")
    return lax.rem(brick, 2), lax.axis_index("slab"), lax.div(brick, 2)


def greet(sizes, me):
    _, slabs, layers = sizes
    core, slab, layer = me
    barrier = pltpu.get_barrier_semaphore()
    peers = [(slab, 2 * layer + 1 - core)]
    peers += [(lax.rem(slab + k, slabs), 2 * layer + core) for k in range(1, slabs)]
    peers += [(slab, 2 * lax.rem(layer + k, layers) + core) for k in range(1, layers)]
    for peer in peers:
        pl.semaphore_signal(barrier, inc=1, device_id=peer, device_id_type=MESH)
    pl.semaphore_wait(barrier, len(peers))


def spread(sizes, me, own, out, sems):
    _, slabs, layers = sizes
    core, slab, layer = me
    a_send, a_recv, b_send, b_recv, c_send, c_recv = sems
    partner = (slab, 2 * layer + 1 - core)
    started = []

    def send(source, target, send_sem, recv_sem, device):
        copy = pltpu.make_async_remote_copy(
            src_ref=source,
            dst_ref=target,
            send_sem=send_sem,
            recv_sem=recv_sem,
            device_id=device,
            device_id_type=MESH,
        )
        copy.start()
        started.append(copy)
        return copy

    def to_slabs(source, target, j):
        return [
            send(
                source,
                target,
                b_send.at[k - 1, j],
                b_recv.at[k - 1, j],
                (lax.rem(slab + k, slabs), 2 * layer + core),
            )
            for k in range(1, slabs)
        ]

    here = out.at[core, slab, layer]
    along = [
        send(own, here, a_send.at[k - 1], a_recv.at[k - 1], (slab, 2 * lax.rem(layer + k, layers) + core))
        for k in range(1, layers)
    ]
    crossing = [to_slabs(own, here, 0)]
    last = [send(own, here, c_send.at[0, 0], c_recv.at[0, 0], partner)]
    for j in range(1, layers):
        along[j - 1].wait_recv()
        block = out.at[core, slab, lax.rem(layer + layers - j, layers)]
        crossing.append(to_slabs(block, block, j))
        last.append(send(block, block, c_send.at[0, j], c_recv.at[0, j], partner))
    for j in range(layers):
        for k in range(1, slabs):
            crossing[j][k - 1].wait_recv()
            block = out.at[
                core, lax.rem(slab + slabs - k, slabs), lax.rem(layer + layers - j, layers)
            ]
            last.append(send(block, block, c_send.at[k, j], c_recv.at[k, j], partner))
    for copy in last:
        copy.wait_recv()
    for copy in started:
        copy.wait_send()


def spread_sems(sizes):
    _, slabs, layers = sizes
    dma = pltpu.SemaphoreType.DMA
    return [
        dma((layers - 1,)),
        dma((layers - 1,)),
        dma((slabs - 1, layers)),
        dma((slabs - 1, layers)),
        dma((slabs, layers)),
        dma((slabs, layers)),
    ]


def gather_kernel(sizes, x, out, local_sem, *sems):
    me = place()
    core, slab, layer = me
    keep = pltpu.make_async_copy(x, out.at[core, slab, layer], local_sem)
    keep.start()
    greet(sizes, me)
    spread(sizes, me, x, out, sems)
    keep.wait()


def gather(block, collective_id):
    sizes = dims()
    return pl.pallas_call(
        functools.partial(gather_kernel, sizes),
        out_shape=jax.ShapeDtypeStruct(sizes + block.shape, block.dtype),
        in_specs=[VM],
        out_specs=VM,
        scratch_shapes=[pltpu.SemaphoreType.DMA] + spread_sems(sizes),
        compiler_params=pltpu.CompilerParams(collective_id=collective_id, has_side_effects=True),
    )(block)


def reduce_kernel(sizes, x, out, first, half, second, quarter, third, *sems):
    cs, cr, ss, sr, zs, zr = sems[:6]
    _, slabs, layers = sizes
    me = place()
    core, slab, layer = me
    greet(sizes, me)

    def send(source, target, send_sem, recv_sem, device):
        copy = pltpu.make_async_remote_copy(
            src_ref=source,
            dst_ref=target,
            send_sem=send_sem,
            recv_sem=recv_sem,
            device_id=device,
            device_id_type=MESH,
        )
        copy.start()
        return copy

    order = list(range(1, slabs)) + [0]
    stage = {}
    for k in order:
        to = lax.rem(slab + k, slabs)
        stage[k] = send(
            x.at[1 - core, to], first.at[to], cs.at[k], cr.at[k], (slab, 2 * layer + 1 - core)
        )
    over = []
    for k in order:
        to = lax.rem(slab + k, slabs)
        stage[k].wait_recv()
        half[to] = x[core, to] + first[to]
        if k:
            over.append(
                send(half.at[to], second.at[k - 1], ss.at[k - 1], sr.at[k - 1], (to, 2 * layer + core))
            )
    total = half[slab]
    for k in range(1, slabs):
        over[k - 1].wait_recv()
        total = total + second[k - 1]
    quarter[...] = total
    along = []
    for k in range(1, layers):
        to = lax.rem(layer + k, layers)
        along.append(
            send(quarter.at[to], third.at[k - 1], zs.at[k - 1], zr.at[k - 1], (slab, 2 * to + core))
        )
    total = quarter[layer]
    for k in range(1, layers):
        along[k - 1].wait_recv()
        total = total + third[k - 1]
    out[core, slab, layer] = total
    spread(sizes, me, out.at[core, slab, layer], out, sems[6:])
    for copy in list(stage.values()) + over + along:
        copy.wait_send()


def all_reduce(rows, collective_id):
    sizes = dims()
    _, slabs, layers = sizes
    devices = 2 * slabs * layers
    count, width = rows.shape
    share = -(-count // devices)
    padded = jnp.pad(rows, ((0, share * devices - count), (0, 0)))
    block = (share, width)
    dma = pltpu.SemaphoreType.DMA
    buffers = [
        (slabs, layers) + block,
        (slabs, layers) + block,
        (slabs - 1, layers) + block,
        (layers,) + block,
        (layers - 1,) + block,
    ]
    result = pl.pallas_call(
        functools.partial(reduce_kernel, sizes),
        out_shape=jax.ShapeDtypeStruct(sizes + block, rows.dtype),
        in_specs=[VM],
        out_specs=VM,
        scratch_shapes=[pltpu.VMEM(item, rows.dtype) for item in buffers]
        + [
            dma((slabs,)),
            dma((slabs,)),
            dma((slabs - 1,)),
            dma((slabs - 1,)),
            dma((layers - 1,)),
            dma((layers - 1,)),
        ]
        + spread_sems(sizes),
        compiler_params=pltpu.CompilerParams(collective_id=collective_id, has_side_effects=True),
    )(padded.reshape(sizes + block))
    return result.reshape(share * devices, width)[:count]


def velocities(indices):
    spacing = 2.0 * VMAX / NVX
    first_index = indices // (NVX * NVX)
    second = indices // NVX % NVX
    third_index = indices % NVX
    coords = jnp.stack([first_index, second, third_index]).astype(jnp.float32)
    return -VMAX + (coords + 0.5) * spacing


def cell_state(vectors, coeffs):
    moments = lax.dot_general(vectors, coeffs, (((1,), (1,)), ((), ())), precision=PRECISE)
    density = jnp.maximum(moments[0], RHO_MIN)
    drift = moments[1:4] / density[None, :]
    temper = jnp.maximum((moments[4] / density - jnp.sum(drift * drift, axis=0)) / 3.0, TEMP_MIN)
    amplitude = density * (2.0 * math.pi * temper) ** (-1.5)
    zero = jnp.zeros_like(density)
    return jnp.stack([drift[0], drift[1], drift[2], -0.5 / temper, amplitude, zero, zero, zero])


def halves(values):
    high = values.astype(jnp.bfloat16)
    return high, (values - high.astype(jnp.float32)).astype(jnp.bfloat16)


def split_into(values, high_low):
    high, low = halves(values)
    rank = values.shape[1]
    high_low[:, :rank] = high
    high_low[:, rank:] = low


def project_kernel(weight, cells, velocity, v_basis, out, high_low):
    @pl.when(pl.program_id(0) == 0)
    def _():
        split_into(v_basis[...], high_low)

    u1, u2, u3 = cells[:, 0:1], cells[:, 1:2], cells[:, 2:3]
    rate, amplitude = cells[:, 3:4], cells[:, 4:5]
    v1, v2, v3 = velocity[0:1, :], velocity[1:2, :], velocity[2:3, :]
    distance = (v1 - u1) ** 2 + (v2 - u2) ** 2 + (v3 - u3) ** 2
    top, rest = halves(jnp.exp(distance * rate))
    both = jnp.dot(top, high_low[...], preferred_element_type=jnp.float32)
    rank = out.shape[1]
    small = jnp.dot(rest, high_low[:, :rank], preferred_element_type=jnp.float32)
    out[...] = (both[:, :rank] + (both[:, rank:] + small)) * (amplitude * weight)


def project(cells, velocity, v_basis, weight):
    count = cells.shape[0]
    nodes, rank = v_basis.shape
    block = math.gcd(count, 256)
    return pl.pallas_call(
        functools.partial(project_kernel, weight),
        grid=(count // block,),
        out_shape=jax.ShapeDtypeStruct((count, rank), jnp.float32),
        in_specs=[
            pl.BlockSpec((block, 8), lambda i: (i, 0)),
            pl.BlockSpec((8, nodes), lambda i: (0, 0)),
            pl.BlockSpec((nodes, rank), lambda i: (0, 0)),
        ],
        out_specs=pl.BlockSpec((block, rank), lambda i: (i, 0)),
        scratch_shapes=[pltpu.VMEM((nodes, 2 * rank), jnp.bfloat16)],
    )(cells, velocity, v_basis)


def fold_kernel(group, weight, cells, velocity, field, out, high_low):
    i = pl.program_id(0)

    @pl.when(i == 0)
    def _():
        out[...] = jnp.zeros_like(out)

    split_into(field[...], high_low)
    u1, u2, u3 = cells[0:1, :], cells[1:2, :], cells[2:3, :]
    rate = cells[3:4, :]
    nodes, rank = out.shape
    fast = jnp.exp(((velocity[0:group, 2:3] - u3) ** 2) * rate)
    pieces = []
    for start in range(0, nodes, group):
        v1 = velocity[start : start + 1, 0:1]
        v2 = velocity[start : start + 1, 1:2]
        slow = jnp.exp(((v1 - u1) ** 2 + (v2 - u2) ** 2) * rate)
        pieces.append(fast * slow)
    top, rest = halves(jnp.concatenate(pieces, axis=0))
    both = jnp.dot(top, high_low[...], preferred_element_type=jnp.float32)
    small = jnp.dot(rest, high_low[:, :rank], preferred_element_type=jnp.float32)
    out[...] += (both[:, :rank] + (both[:, rank:] + small)) * weight


def fold(cells, velocity, field, weight):
    count, rank = field.shape
    nodes = velocity.shape[0]
    block = math.gcd(count, 256)
    group = math.gcd(nodes, NVX)
    return pl.pallas_call(
        functools.partial(fold_kernel, group, weight),
        grid=(count // block,),
        out_shape=jax.ShapeDtypeStruct((nodes, rank), jnp.float32),
        in_specs=[
            pl.BlockSpec((8, block), lambda i: (0, i)),
            pl.BlockSpec((nodes, 8), lambda i: (0, 0)),
            pl.BlockSpec((block, rank), lambda i: (i, 0)),
        ],
        out_specs=pl.BlockSpec((nodes, rank), lambda i: (0, 0)),
        scratch_shapes=[pltpu.VMEM((block, 2 * rank), jnp.bfloat16)],
    )(cells, velocity, field * cells[4][:, None])


def forward_slopes(grid, lengths):
    return [(jnp.roll(grid, -1, axis=d) - grid) * lengths[d] for d in range(3)]


def factor_kernel(matrix, factor, inverse, work):
    size = matrix.shape[0]
    panel = 8
    row = lax.broadcasted_iota(jnp.int32, (size, size), 0)
    column = lax.broadcasted_iota(jnp.int32, (size, size), 1)
    work[:, :size] = matrix[...]
    work[:, size:] = jnp.where(row == column, 1.0, 0.0)
    wide = (panel, 2 * size)
    sub = lax.broadcasted_iota(jnp.int32, wide, 0)
    sub_one = lax.broadcasted_iota(jnp.int32, (panel, size), 0)
    for start in range(0, size, panel):
        rows = work[start : start + panel, :]
        columns = [
            jnp.broadcast_to(rows[:, start + k : start + k + 1], (panel, size))
            for k in range(panel)
        ]
        for k in range(panel):
            scale = lax.rsqrt(columns[k][k : k + 1, :])
            ratio = columns[k] * (scale * scale)
            ratio = jnp.where(sub_one > k, ratio, jnp.where(sub_one == k, 1.0 - scale, 0.0))
            for m in range(k + 1, panel):
                columns[m] = columns[m] - ratio * columns[m][k : k + 1, :]
            rows = rows - jnp.concatenate([ratio, ratio], axis=1) * rows[k : k + 1, :]
        work[start : start + panel, :] = rows
        if start + panel < size:
            tall = rows[:, :size].T[start + panel :, :]
            work[start + panel :, :] = work[start + panel :, :] - jnp.dot(
                tall, rows, precision=PRECISE, preferred_element_type=jnp.float32
            )
    factor[...] = jnp.where(column <= row, work[:, :size].T, 0.0)
    inverse[...] = jnp.where(column <= row, work[:, size:], 0.0)


def factor_and_inverse(matrix):
    shape = jax.ShapeDtypeStruct(matrix.shape, matrix.dtype)
    size = matrix.shape[0]
    return pl.pallas_call(
        factor_kernel,
        out_shape=(shape, shape),
        in_specs=[VM],
        out_specs=(VM, VM),
        scratch_shapes=[pltpu.VMEM((size, 2 * size), jnp.float32)],
    )(matrix)


def products_kernel(depth, here, after, mproj, out):
    @pl.when(pl.program_id(0) == 0)
    def _():
        out[...] = jnp.zeros_like(out)

    field = here[...]
    count, rank = field.shape
    up_second = jnp.concatenate([field[depth:], field[:depth]], axis=0)
    index = lax.broadcasted_iota(jnp.int32, field.shape, 0)
    up_third = jnp.where(
        lax.rem(index, depth) == depth - 1,
        pltpu.roll(field, depth - 1, 0),
        pltpu.roll(field, count - 1, 0),
    )
    right = jnp.concatenate(
        [after[...] - field, up_second - field, up_third - field, mproj[...], field], axis=1
    )
    high, low = halves(right)
    left_high, left_low = halves(field.T)
    out[...] += (
        jnp.dot(left_high, high, preferred_element_type=jnp.float32)
        + jnp.dot(left_high, low, preferred_element_type=jnp.float32)
        + jnp.dot(left_low, high, preferred_element_type=jnp.float32)
    )


def products(field, mproj, lengths):
    rank = field.shape[1]
    plane = lengths[1] * lengths[2]
    block = (plane, rank)
    return pl.pallas_call(
        functools.partial(products_kernel, lengths[2]),
        grid=(lengths[0],),
        out_shape=jax.ShapeDtypeStruct((rank, 5 * rank), jnp.float32),
        in_specs=[
            pl.BlockSpec(block, lambda i: (i, 0)),
            pl.BlockSpec(block, lambda i: (lax.rem(i + 1, lengths[0]), 0)),
            pl.BlockSpec(block, lambda i: (i, 0)),
        ],
        out_specs=pl.BlockSpec((rank, 5 * rank), lambda i: (0, 0)),
    )(field, field, mproj)


def small_kernel(sizes, x, out, first, second, *sems):
    ms, mr, zs, zr, gs, gr = sems
    _, slabs, layers = sizes
    core, slab, layer = place()
    members = 2 * slabs
    me = 2 * slab + core

    def member(k):
        to = lax.rem(me + k, members)
        return to, (lax.div(to, 2), 2 * layer + lax.rem(to, 2))

    def across(k):
        return (slab, 2 * lax.rem(layer + k, layers) + core)

    barrier = pltpu.get_barrier_semaphore()
    peers = [member(k)[1] for k in range(1, members)] + [across(k) for k in range(1, layers)]
    for peer in peers:
        pl.semaphore_signal(barrier, inc=1, device_id=peer, device_id_type=MESH)
    pl.semaphore_wait(barrier, len(peers))

    def send(source, target, send_sem, recv_sem, device):
        copy = pltpu.make_async_remote_copy(
            src_ref=source,
            dst_ref=target,
            send_sem=send_sem,
            recv_sem=recv_sem,
            device_id=device,
            device_id_type=MESH,
        )
        copy.start()
        return copy

    scatter = []
    for k in range(1, members):
        to, device = member(k)
        scatter.append(send(x.at[to], first.at[k - 1], ms.at[k - 1], mr.at[k - 1], device))
    total = x[me]
    for k in range(1, members):
        scatter[k - 1].wait_recv()
        total = total + first[k - 1]
    second[layer] = total
    mine = second.at[layer]
    cross = [
        send(mine, mine, zs.at[k - 1], zr.at[k - 1], across(k)) for k in range(1, layers)
    ]
    for copy in cross:
        copy.wait_recv()
    total = second[0]
    for k in range(1, layers):
        total = total + second[k]
    out[me] = total
    mine = out.at[me]
    collect = [
        send(mine, mine, gs.at[k - 1], gr.at[k - 1], member(k)[1]) for k in range(1, members)
    ]
    for copy in collect:
        copy.wait_recv()
    for copy in scatter + cross + collect:
        copy.wait_send()


def small_all_reduce(rows, collective_id):
    sizes = dims()
    _, slabs, layers = sizes
    members = 2 * slabs
    count, width = rows.shape
    share = -(-count // members)
    padded = jnp.pad(rows, ((0, share * members - count), (0, 0)))
    dma = pltpu.SemaphoreType.DMA
    result = pl.pallas_call(
        functools.partial(small_kernel, sizes),
        out_shape=jax.ShapeDtypeStruct((members, share, width), rows.dtype),
        in_specs=[VM],
        out_specs=VM,
        scratch_shapes=[
            pltpu.VMEM((members - 1, share, width), rows.dtype),
            pltpu.VMEM((layers, share, width), rows.dtype),
            dma((members - 1,)),
            dma((members - 1,)),
            dma((layers - 1,)),
            dma((layers - 1,)),
            dma((members - 1,)),
            dma((members - 1,)),
        ],
        compiler_params=pltpu.CompilerParams(collective_id=collective_id, has_side_effects=True),
    )(padded.reshape(members, share, width))
    return result.reshape(share * members, width)[:count]


def local(k_coeffs, v_basis):
    cells_x, cells_y, cells_z, rank = k_coeffs.shape
    slabs = lax.axis_size("slab")
    bricks = lax.axis_size("brick")
    lengths = (cells_x * slabs, cells_y * bricks, cells_z)
    cells = lengths[0] * lengths[1] * lengths[2]
    time_step = CFL / (VMAX * (lengths[0] + lengths[1] + lengths[2]))
    weight_x = 1.0 / cells
    weight_v = (2.0 * VMAX / NVX) ** 3
    nodes = v_basis.shape[0]
    slab, brick = lax.axis_index("slab"), lax.axis_index("brick")
    row_ids = (slab * bricks + brick) * nodes + jnp.arange(nodes, dtype=jnp.int32)
    velocity = velocities(row_ids)
    positive = jnp.maximum(velocity, 0.0)
    negative = jnp.minimum(velocity, 0.0)
    square = jnp.sum(velocity * velocity, axis=0)
    zero = jnp.zeros_like(square)
    ones = jnp.ones_like(square)
    weights = jnp.stack([ones, velocity[0], velocity[1], velocity[2], square, zero, zero, zero])
    partial = jnp.dot(weights, v_basis, precision=PRECISE) * weight_v
    packed = jnp.concatenate([partial, k_coeffs.reshape(-1, rank)], axis=0)
    gathered = gather(packed, 1)
    vectors = jnp.sum(gathered[:, :, :, :8], axis=(0, 1, 2))
    blocks = gathered[:, :, :, 8:].reshape(2, slabs, bricks // 2, cells_x, cells_y, cells_z, rank)
    grid = blocks.transpose(1, 3, 2, 0, 4, 5, 6).reshape(lengths + (rank,))
    flat = grid.reshape(cells, rank)

    rows = cell_state(vectors, flat)
    velocity_rows = jnp.pad(velocity, ((0, 5), (0, 0)))
    mproj_part = project(rows.T, velocity_rows, v_basis, weight_v)
    sides = jnp.concatenate([positive, negative], axis=0) * weight_v
    transport_part = lax.dot_general(
        sides[:, :, None] * v_basis[None],
        v_basis,
        (((1,), (0,)), ((), ())),
        precision=FAST,
    )
    summed = all_reduce(jnp.concatenate([mproj_part, transport_part.reshape(6 * rank, rank)]), 2)
    mproj = summed[:cells]
    transport = summed[cells:]

    fwd = forward_slopes(grid, lengths)
    back = [jnp.roll(item, 1, axis=d) for d, item in enumerate(fwd)]
    flux = sum(
        jnp.dot(item.reshape(cells, rank), transport[k * rank : (k + 1) * rank], precision=FAST)
        for k, item in enumerate(back + fwd)
    )
    advanced = flat - time_step * flux + COLLIDE * (mproj - flat)

    new_grid = advanced.reshape(lengths + (rank,))
    over_cells = (((0,), (0,)), ((), ()))
    sums = products(advanced, mproj, lengths)
    raw = [sums[:, k * rank : (k + 1) * rank] for k in range(5)]
    slopes_raw = jnp.stack([raw[d] * (lengths[d] * weight_x) for d in range(3)])
    factor, inverse = factor_and_inverse(raw[4] * weight_x)
    plus = jnp.einsum("ab,kbc,dc->kad", inverse, slopes_raw, inverse, precision=PRECISE)
    minus = -plus.transpose(0, 2, 1)
    projected = jnp.dot(inverse, raw[3] * weight_x, precision=PRECISE)
    both = jnp.concatenate([minus, plus], axis=0)
    middle = jnp.einsum("kab,cb->akc", both, factor, precision=PRECISE).reshape(rank, 6 * rank)
    hat = factor.T
    coupling_mid = (
        hat
        + time_step * jnp.dot(middle, transport, precision=PRECISE)
        - COLLIDE * (projected - hat)
    )

    velocity_columns = velocity_rows.T
    back_raw = fold(rows, velocity_columns, advanced, weight_x)
    back_proj = lax.dot_general(back_raw, inverse, (((1,), (1,)), ((), ())), precision=FAST)
    lnow = lax.dot_general(v_basis, coupling_mid, (((1,), (1,)), ((), ())), precision=FAST)
    turned = both.transpose(2, 0, 1).reshape(rank, 6 * rank)
    moved = jnp.dot(lnow, turned, precision=FAST)
    side_columns = jnp.concatenate([positive, negative], axis=0).T
    drift = sum(
        side_columns[:, k : k + 1] * moved[:, k * rank : (k + 1) * rank] for k in range(6)
    )
    lnew = lnow - time_step * drift + COLLIDE * (back_proj - lnow)
    gram_v = lax.dot_general(lnew, lnew, over_cells, precision=PRECISE) * weight_v
    gram_v = small_all_reduce(gram_v, 3)
    coupling, inverse_v = factor_and_inverse(gram_v)
    basis_v = lax.dot_general(lnew, inverse_v, (((1,), (1,)), ((), ())), precision=FAST)
    own = lax.dynamic_slice(
        new_grid,
        (slab * cells_x, brick * cells_y, 0, 0),
        (cells_x, cells_y, cells_z, rank),
    ).reshape(-1, rank)
    basis_x = lax.dot_general(own, inverse, (((1,), (1,)), ((), ())), precision=FAST)
    return basis_x.reshape(k_coeffs.shape), coupling, basis_v


def solution(mesh):
    return jax.shard_map(
        local,
        mesh=mesh,
        in_specs=(P("slab", "brick", None, None), P(("slab", "brick"), None)),
        out_specs=(P("slab", "brick", None, None), P(), P(("slab", "brick"), None)),
        check_vma=False,
    )
```

profile of v0, /device:TPU:0, one launch (start us, length us, event | category | flops | bytes accessed | tf_op | source)
XLA Modules:
  0.0 142.1 jit_solution(3373837350839305605)
XLA Ops:
  3.0 17.8 %shard_map.49 = f32[2,4,4,72,128]{4,3,2,1,0:T(8,128)} custom-call(f32[72,128]{1,0:T(8,128)} %pad_maximum_fusion.8.x), custom_call_target="tpu_custom_call" | custom-call | tf_op jit(solution)/shard_map/pallas_call | solution.py:127
  20.8 1.0 slice_reduce_fusion
  22.2 1.0 fusion.60
  23.3 1.0 copy.62
  24.7 2.4 %fusion = f32[6,128,128]{2,1,0:T(8,128)S(1)} fusion(f32[1024,128]{0,1:T(8,128)} %copy.62, f32[6,1024]{1,0:T(8,128)S(1)} %get-tuple-element.42, f32[1024,128]{1,0:T(8,128)S(1)} %copy-done), kind=kOutput, calls=%fused_computation | convolution fusion | flops 604766208 | bytes 1466368 | tf_op jit(solution)/shard_map/dot_general | solution.py:549
  27.3 1.3 copy.58.cells
  29.2 8.5 %shard_map.50 = f32[2048,128]{1,0:T(8,128)} custom-call(f32[2048,8]{1,0:T(8,128)} %copy.58.cells, f32[8,1024]{1,0:T(8,128)} %pad.4.clone.velocity, f32[1024,128]{1,0:T(8,128)} %v_basis.1), custom_call_target="tpu_custom_call" | custom-call | tf_op jit(solution)/shard_map/pallas_call | solution.py:280
  37.8 2.4 %pad_maximum_fusion = f32[2816,128]{1,0:T(8,128)} fusion(f32[768,128]{1,0:T(8,128)S(1)} %bitcast.132, f32[2048,128]{1,0:T(8,128)} %shard_map.50), kind=kLoop, calls=%fused_computation.12 | loop fusion | flops 360448 | bytes 2883584 | tf_op jit(solution)/shard_map/concatenate | solution.py:555
  40.2 33.6 %shard_map.51 = f32[2,4,4,88,128]{4,3,2,1,0:T(8,128)} custom-call(f32[2,4,4,88,128]{4,3,2,1,0:T(8,128)} %bitcast.123), custom_call_target="tpu_custom_call" | custom-call | tf_op jit(solution)/shard_map/pallas_call | solution.py:209
  75.1 1.3 copy-done.2
  80.0 2.0 %broadcast_multiply_fusion = (f32[2048,128]{1,0:T(8,128)}, f32[2048,128]{1,0:T(8,128)}) fusion(f32[2048]{0:T(1024)S(1)} %power_multiply_fusion, f32[2048,128]{1,0:T(8,128)S(1)} %bitcast.113, f32[2816,128]{1,0:T(8,128)S(1)} %bitcast.120, f32[2048,128]{1,0:T(8,128)S(1)} %convolution_add_fusion.1, f32[2048,128]{1,0:T(8,128)S(1)} %get-tuple-element.17), kind=kOutput, calls=%fused_computation.52 | convolution fusion | flops 203161600 | bytes 6365184 | tf_op jit(solution)/shard_map/dot_general | solution.py:562
  82.0 1.0 slice.215.mproj
  83.0 6.9 %shard_map.52 = f32[128,640]{1,0:T(8,128)} custom-call(f32[2048,128]{1,0:T(8,128)} %get-tuple-element.44.here.after, f32[2048,128]{1,0:T(8,128)} %get-tuple-element.44.here.after, f32[2048,128]{1,0:T(8,128)} %slice.215.mproj), custom_call_target="tpu_custom_call" | custom-call | tf_op jit(solution)/shard_map/pallas_call | solution.py:416
  90.0 1.6 %fusion.32 = (f32[1,128,128]{2,1,0:T(8,128)S(1)}, f32[1,128,128]{2,1,0:T(8,128)S(1)}, f32[1,128,128]{2,1,0:T(8,128)S(1)}, f32[128,128]{1,0:T(8,128)}) fusion(f32[128,640]{1,0:T(8,128)} %shard_map.52), kind=kLoop, calls=%fused_computation.73 | loop fusion | flops 65536 | bytes 524288 | tf_op jit(solution)/shard_map/stack | solution.py:571
  91.5 8.9 %shard_map.53 = (f32[128,128]{1,0:T(8,128)}, f32[128,128]{1,0:T(8,128)}) custom-call(f32[128,128]{1,0:T(8,128)} %get-tuple-element.33.matrix), custom_call_target="tpu_custom_call" | custom-call | tf_op jit(solution)/shard_map/pallas_call | solution.py:377
  100.4 1.7 %fusion.40 = f32[2,2,16,128]{3,2,1,0:T(8,128)} fusion(f32[128,128]{1,0:T(8,128)} %get-tuple-element.7, f32[8,16,16,128]{3,2,1,0:T(8,128)} %bitcast.114, s32[]{:T(128)S(6)} %select_n.57, s32[]{:T(128)S(6)} %select_n.58), kind=kOutput, calls=%fused_computation.82 | convolution fusion | flops 6291456 | bytes 131080 | tf_op jit(solution)/shard_map/dot_general | solution.py:605
  102.1 0.8 pad_bitcast_fusion.velocity
  102.9 7.5 %shard_map.54 = f32[1024,128]{1,0:T(8,128)} custom-call(f32[8,2048]{1,0:T(8,128)} %copy-done.5, f32[1024,8]{1,0:T(8,128)} %pad_bitcast_fusion.velocity, f32[2048,128]{1,0:T(8,128)} %get-tuple-element.43.field), custom_call_target="tpu_custom_call" | custom-call | tf_op jit(solution)/shard_map/pallas_call | solution.py:323
  112.5 1.1 fusion.10
  114.1 1.4 fusion.62
  116.2 1.2 convolution_multiply_fusion
  117.4 13.6 %shard_map.55 = f32[8,16,128]{2,1,0:T(8,128)} custom-call(f32[8,16,128]{2,1,0:T(8,128)} %bitcast.133), custom_call_target="tpu_custom_call" | custom-call | tf_op jit(solution)/shard_map/pallas_call | solution.py:498
  131.0 8.9 %shard_map.56 = (f32[128,128]{1,0:T(8,128)}, f32[128,128]{1,0:T(8,128)}) custom-call(f32[128,128]{1,0:T(8,128)} %bitcast.134), custom_call_target="tpu_custom_call" | custom-call | tf_op jit(solution)/shard_map/pallas_call | solution.py:377
  139.9 2.2 %fusion.63 = f32[1024,128]{1,0:T(8,128)} fusion(f32[1024,128]{0,1:T(8,128)S(1)} %fusion.8, f32[128,128]{1,0:T(8,128)} %get-tuple-element.10), kind=kOutput, calls=%fused_computation.128 | convolution fusion | flops 100663296 | bytes 1114112 | tf_op jit(solution)/shard_map/dot_general | solution.py:599
  (73 shorter events, 11.8 us)
Async XLA Ops:
  1.0 1.0 copy-start
  1.0 1.4 copy-start.7
  20.8 1.3 slice-start
  27.3 10.5 %copy-start.5 = (f32[8,2048]{1,0:T(8,128)}, f32[8,2048]{1,0:T(8,128)S(1)}, u32[]{:S(2)}) copy-start(f32[8,2048]{1,0:T(8,128)S(1)} %stack.41.cells) | copy-start | bytes 196612
  75.0 1.4 copy-start.2
  102.1 8.3 %copy-start.3 = (f32[128,128]{1,0:T(8,128)S(1)}, f32[128,128]{1,0:T(8,128)}, u32[]{:S(2)}) copy-start(f32[128,128]{1,0:T(8,128)} %get-tuple-element.7) | copy-start | bytes 196612
  102.9 8.3 %copy-start.4 = (f32[128,128]{1,0:T(8,128)S(1)}, f32[128,128]{1,0:T(8,128)}, u32[]{:S(2)}) copy-start(f32[128,128]{1,0:T(8,128)} %get-tuple-element.8) | copy-start | bytes 196612
  111.1 2.6 %copy-start.1 = (f32[1024,128]{1,0:T(8,128)S(1)}, f32[1024,128]{1,0:T(8,128)}, u32[]{:S(2)}) copy-start(f32[1024,128]{1,0:T(8,128)} %v_basis.1) | copy-start | bytes 1572868
  114.1 1.4 %copy-start.6 = (f32[1024,128]{1,0:T(8,128)S(1)}, f32[1024,128]{1,0:T(8,128)}, u32[]{:S(2)}) copy-start(f32[1024,128]{1,0:T(8,128)} %shard_map.54) | copy-start | bytes 1572868
where the time goes:
time: 143 us; the launch traced here: 142 us
  Pallas kernels  106 us (74%)
  matrix products  19.2 us (13%)
  local copies, waits for them, and re-layouts  8.52 us (6%)
  other arithmetic  7.53 us (5%)
    pallas_call x1, Pallas kernels, all_reduce(): pl.pallas_call(functools.partial(reduce_kernel, sizes), out_shape=jax.Sha...  33.6 us
    pallas_call x1, Pallas kernels, gather(): pl.pallas_call(functools.partial(gather_kernel, sizes), out_shape=jax.Sha...  17.8 us
    pallas_call x2, Pallas kernels, factor_and_inverse(): pl.pallas_call(factor_kernel, out_shape=(shape, shape), in_specs=[VM], ou...  17.8 us
    pallas_call x1, Pallas kernels, small_all_reduce(): pl.pallas_call(functools.partial(small_kernel, sizes), out_shape=jax.Shap...  13.6 us
    pallas_call x1, Pallas kernels, project(): pl.pallas_call(functools.partial(project_kernel, weight), grid=(count //...  8.54 us
    pallas_call x1, Pallas kernels, fold(): pl.pallas_call(functools.partial(fold_kernel, group, weight), grid=(count...  7.47 us
    pallas_call x1, Pallas kernels, products(): pl.pallas_call(functools.partial(products_kernel, lengths[2]), grid=(leng...  6.94 us
    dot_general x6, matrix products, local(): jnp.dot(item.reshape(cells, rank), transport[k * rank:(k + 1) * rank], pr...  4.92 us

commit v1 on v0

v1 whole, which is shorter than its diff:
```python
import functools
import math

import jax
import jax.numpy as jnp
from jax import lax
from jax.experimental import pallas as pl
from jax.experimental.pallas import tpu as pltpu
from jax.sharding import PartitionSpec as P

NVX = 32

CFL = 0.9
VMAX = 6.0
COLLIDE = 0.3
RHO_MIN = 0.25
TEMP_MIN = 0.25
PRECISE = lax.Precision.HIGHEST
MESH = pl.DeviceIdType.MESH
VM = pl.BlockSpec(memory_space=pltpu.VMEM)
F32 = jnp.float32
BF16 = jnp.bfloat16
BITS = NVX.bit_length() - 1


def halves(values):
    high = values.astype(BF16)
    return high, (values - high.astype(F32)).astype(BF16)


def dot(left, right):
    return jnp.dot(left, right, preferred_element_type=F32)


def dot_split(high, low, right):
    width = right.shape[1]
    right_high, right_low = halves(right)
    both = dot(high, jnp.concatenate([right_high, right_low], axis=1))
    return both[:, :width] + (both[:, width:] + dot(low, right_high))


def dot3(left, right):
    return dot_split(*halves(left), right)


def dot6(left, right):
    return jnp.dot(left, right, precision=PRECISE, preferred_element_type=F32)


def node_velocity(indices):
    spacing = 2.0 * VMAX / NVX
    last = NVX - 1
    parts = (
        lax.shift_right_logical(indices, 2 * BITS),
        lax.shift_right_logical(indices, BITS) & last,
        indices & last,
    )
    return [-VMAX + (part.astype(F32) + 0.5) * spacing for part in parts]


class Sum:
    def __init__(self, send, pos, x, first, second, out, sems):
        self.send, self.pos = send, pos
        self.x, self.first, self.second, self.out = x, first, second, out
        self.sems = sems

    def scatter(self):
        me, members, member = self.pos.me, self.pos.members, self.pos.member
        self.copies = []
        for k in range(1, members):
            to, device = member(k)
            self.copies.append(
                self.send(
                    self.x.at[to], self.first.at[k - 1], self.sems[0].at[k - 1], self.sems[1].at[k - 1], device
                )
            )

    def cross(self):
        me, layer = self.pos.me, self.pos.layer
        total = self.x[me]
        for k, copy in enumerate(self.copies):
            copy.wait_recv()
            total = total + self.first[k]
        self.second[layer] = total
        mine = self.second.at[layer]
        self.copies = [
            self.send(mine, mine, self.sems[2].at[k - 1], self.sems[3].at[k - 1], self.pos.across(k))
            for k in range(1, self.pos.layers)
        ]

    def collect(self):
        me = self.pos.me
        for copy in self.copies:
            copy.wait_recv()
        total = self.second[0]
        for k in range(1, self.pos.layers):
            total = total + self.second[k]
        self.out[me] = total
        mine = self.out.at[me]
        self.copies = [
            self.send(mine, mine, self.sems[4].at[k - 1], self.sems[5].at[k - 1], self.pos.member(k)[1])
            for k in range(1, self.pos.members)
        ]

    def finish(self):
        for copy in self.copies:
            copy.wait_recv()


class Position:
    def __init__(self, slabs, layers):
        self.slabs, self.layers, self.members = slabs, layers, 2 * slabs
        brick = lax.axis_index("brick")
        self.brick = brick
        self.core, self.layer = lax.rem(brick, 2), lax.div(brick, 2)
        self.slab = lax.axis_index("slab")
        self.me = 2 * self.slab + self.core

    def member(self, k):
        to = lax.rem(self.me + k, self.members)
        return to, (lax.div(to, 2), 2 * self.layer + lax.rem(to, 2))

    def across(self, k):
        return (self.slab, 2 * lax.rem(self.layer + k, self.layers) + self.core)

    def partner(self):
        return (self.slab, 2 * self.layer + 1 - self.core)

    def slab_at(self, k):
        to = lax.rem(self.slab + k, self.slabs)
        return to, (to, self.brick)

    def brick_at(self, k):
        bricks = 2 * self.layers
        return (self.slab, lax.rem(self.brick + k + bricks, bricks))


def factor_steps(work, matrix):
    size = matrix.shape[0]
    panel = 8
    row = lax.broadcasted_iota(jnp.int32, (size, size), 0)
    column = lax.broadcasted_iota(jnp.int32, (size, size), 1)
    work[:, :size] = matrix
    work[:, size:] = jnp.where(row == column, 1.0, 0.0)
    sub_one = lax.broadcasted_iota(jnp.int32, (panel, size), 0)
    for start in range(0, size, panel):
        rows = work[start : start + panel, :]
        columns = [
            jnp.broadcast_to(rows[:, start + k : start + k + 1], (panel, size))
            for k in range(panel)
        ]
        for k in range(panel):
            scale = lax.rsqrt(columns[k][k : k + 1, :])
            ratio = columns[k] * (scale * scale)
            ratio = jnp.where(sub_one > k, ratio, jnp.where(sub_one == k, 1.0 - scale, 0.0))
            for m in range(k + 1, panel):
                columns[m] = columns[m] - ratio * columns[m][k : k + 1, :]
            rows = rows - jnp.concatenate([ratio, ratio], axis=1) * rows[k : k + 1, :]
        work[start : start + panel, :] = rows
        if start + panel < size:
            tall = rows[:, :size].T[start + panel :, :]
            work[start + panel :, :] = work[start + panel :, :] - jnp.dot(
                tall, rows, precision=PRECISE, preferred_element_type=F32
            )
    factor = jnp.where(column <= row, work[:, :size].T, 0.0)
    inverse = jnp.where(column <= row, work[:, size:], 0.0)
    return factor, inverse


def step_kernel(names, slabs, layers, *refs):
    ref = dict(zip(names, refs))
    pos = Position(slabs, layers)
    core, slab, layer, brick, me = pos.core, pos.slab, pos.layer, pos.brick, pos.me
    members, bricks = pos.members, 2 * layers
    k_ref, v_ref = ref["k"], ref["v"]
    cells_x, cells_y, cells_z, rank = k_ref.shape
    own = cells_x * cells_y * cells_z
    nodes = v_ref.shape[0]
    lengths = (cells_x * slabs, cells_y * bricks, cells_z)
    cells = lengths[0] * lengths[1] * lengths[2]
    time_step = CFL / (VMAX * (lengths[0] + lengths[1] + lengths[2]))
    weight_x = 1.0 / cells
    weight_v = (2.0 * VMAX / NVX) ** 3
    base = (slab * bricks + brick) * nodes
    started = []

    def send(source, target, send_sem, recv_sem, device):
        copy = pltpu.make_async_remote_copy(
            src_ref=source,
            dst_ref=target,
            send_sem=send_sem,
            recv_sem=recv_sem,
            device_id=device,
            device_id_type=MESH,
        )
        copy.start()
        started.append(copy)
        return copy

    barrier = pltpu.get_barrier_semaphore()
    peers = [pos.member(k)[1] for k in range(1, members)]
    peers += [pos.across(k) for k in range(1, layers)]
    peers += [pos.brick_at(1), pos.brick_at(-1)]
    for peer in peers:
        pl.semaphore_signal(barrier, inc=1, device_id=peer, device_id_type=MESH)

    lane = lax.broadcasted_iota(jnp.int32, (8, nodes), 1)
    sub = lax.broadcasted_iota(jnp.int32, (8, nodes), 0)
    velocity = node_velocity(base + lane)
    square = velocity[0] * velocity[0] + velocity[1] * velocity[1] + velocity[2] * velocity[2]
    weights = jnp.where(sub == 0, 1.0, jnp.where(sub == 4, square, 0.0))
    upward = jnp.zeros_like(weights)
    for d in range(3):
        weights = jnp.where(sub == d + 1, velocity[d], weights)
        upward = jnp.where(sub == d + 5, jnp.maximum(velocity[d], 0.0), upward)
    values = v_ref[...]
    v_high, v_low = halves(values)
    v_rest = (values - v_high.astype(F32) - v_low.astype(F32)).astype(BF16)
    sums = dot(jnp.concatenate(halves(weights), axis=0), jnp.concatenate([v_high, v_low, v_rest], axis=1))
    sums = sums[:8] + sums[8:]
    squares = dot(upward.astype(BF16), jnp.concatenate(halves(values * values), axis=1))
    partial = sums[:, :rank] + (sums[:, rank : 2 * rank] + sums[:, 2 * rank :])
    partial = (partial + (squares[:, :rank] + squares[:, rank:])) * weight_v
    vec_l, vec_m = ref["vec_l"], ref["vec_m"]
    vec_l[layer] = partial

    pl.semaphore_wait(barrier, len(peers))
    mine = vec_l.at[layer]
    copies = [
        send(mine, mine, ref["vls"].at[k - 1], ref["vlr"].at[k - 1], pos.across(k)) for k in range(1, layers)
    ]
    halo_a, halo_b = ref["halo_a"], ref["halo_b"]
    halos = [
        send(k_ref.at[cells_x - 1], halo_a.at[0], ref["hs"].at[0], ref["hr"].at[0], pos.slab_at(1)[1]),
        send(k_ref.at[0], halo_a.at[1], ref["hs"].at[1], ref["hr"].at[1], pos.slab_at(slabs - 1)[1]),
        send(k_ref.at[:, cells_y - 1], halo_b.at[0], ref["hs"].at[2], ref["hr"].at[2], pos.brick_at(1)),
        send(k_ref.at[:, 0], halo_b.at[1], ref["hs"].at[3], ref["hr"].at[3], pos.brick_at(-1)),
    ]

    turned_v = values.T
    vt_high, vt_low = halves(turned_v)
    vt = ref["vt"]
    vt[:rank] = vt_high
    vt[rank:] = vt_low
    v_both = jnp.concatenate([v_high, v_low], axis=1)
    row = lax.broadcasted_iota(jnp.int32, (rank, rank), 0)
    column = lax.broadcasted_iota(jnp.int32, (rank, rank), 1)
    packed = []
    for d in range(3):
        sides = []
        for side in (jnp.maximum(velocity[d][:1], 0.0), jnp.minimum(velocity[d][:1], 0.0)):
            high, low = halves(turned_v * (side * weight_v))
            both = dot(high, v_both)
            sides.append(both[:, :rank] + (both[:, rank:] + dot(low, v_high)))
        packed.append(jnp.where(row > column, sides[0], sides[1]))
    share = 3 * rank // members
    ref["tx"][...] = jnp.concatenate(packed, axis=0).reshape(members, share, rank)
    transport_sum = Sum(send, pos, ref["tx"], ref["t1"], ref["t2"], ref["to"], [ref[f"tsem{i}"] for i in range(6)])

    for copy in copies:
        copy.wait_recv()
    total = vec_l[0]
    for k in range(1, layers):
        total = total + vec_l[k]
    vec_m[me] = total
    mine = vec_m.at[me]
    copies = [
        send(mine, mine, ref["vms"].at[k - 1], ref["vmr"].at[k - 1], pos.member(k)[1]) for k in range(1, members)
    ]
    transport_sum.scatter()
    own_k = k_ref[...].reshape(own, rank)
    kpad = ref["kpad"]
    kpad[...] = jnp.zeros_like(kpad)
    kpad[pl.ds(pl.multiple_of(core * own, 8), own), :] = own_k
    for copy in copies:
        copy.wait_recv()
    vectors = vec_m[0]
    for k in range(1, members):
        vectors = vectors + vec_m[k]

    moments = lax.dot_general(
        vectors, kpad[...], (((1,), (1,)), ((), ())), precision=PRECISE, preferred_element_type=F32
    )
    pair = 2 * own
    density = jnp.maximum(moments[0:1], RHO_MIN)
    drift = [moments[d : d + 1] / density for d in range(1, 4)]
    bulk = drift[0] * drift[0] + drift[1] * drift[1] + drift[2] * drift[2]
    temper = jnp.maximum((moments[4:5] / density - bulk) / 3.0, TEMP_MIN)
    wide = 2.0 * math.pi * temper
    amplitude = density / (wide * jnp.sqrt(wide))
    state = jnp.zeros((8, pair), F32)
    sub_pair = lax.broadcasted_iota(jnp.int32, (8, pair), 0)
    lane_pair = lax.broadcasted_iota(jnp.int32, (8, pair), 1)
    for i, item in enumerate(drift + [-0.5 / temper, amplitude]):
        state = jnp.where(sub_pair == i, item, state)
    inside = (lane_pair >= core * own) & (lane_pair < (core + 1) * own)
    par = ref["par"]
    par[me, layer] = jnp.where(inside, state, 0.0)
    mine = par.at[me, layer]
    copies = [
        send(mine, mine, ref["pls"].at[k - 1], ref["plr"].at[k - 1], pos.across(k)) for k in range(1, layers)
    ]
    transport_sum.cross()
    for copy in copies:
        copy.wait_recv()
    mine = par.at[me]
    copies = [
        send(mine, mine, ref["pms"].at[k - 1], ref["pmr"].at[k - 1], pos.member(k)[1]) for k in range(1, members)
    ]
    transport_sum.collect()
    for copy in copies:
        copy.wait_recv()

    mt_high, mt_low = ref["mt_high"], ref["mt_low"]
    mp, first, half, second, third = ref["mp"], ref["first"], ref["half"], ref["second"], ref["third"]
    group = math.gcd(nodes, NVX)
    groups = nodes // group
    width = 2 * pair
    slots = layers // 2
    fast_v = node_velocity(base + lax.broadcasted_iota(jnp.int32, (group, width), 0))
    slow_v = node_velocity(base + group * lax.broadcasted_iota(jnp.int32, (groups, width), 0))

    def project(to, slot):
        blocks = [par[2 * to, 2 * slot + i] + par[2 * to + 1, 2 * slot + i] for i in range(2)]
        state = jnp.concatenate(blocks, axis=1)
        u = [state[d : d + 1] for d in range(3)]
        rate, scale = state[3:4], state[4:5]
        fast = jnp.exp((fast_v[2] - u[2]) ** 2 * rate)
        slow = jnp.exp(((slow_v[0] - u[0]) ** 2 + (slow_v[1] - u[1]) ** 2) * rate) * scale
        place = pl.ds(pl.multiple_of((to * slots + slot) * width, width), width)
        for t in range(groups):
            high, low = halves(fast * slow[t : t + 1])
            mt_high[t * group : (t + 1) * group, place] = high
            mt_low[t * group : (t + 1) * group, place] = low
        high = dot(vt[...], mt_high[:, place])
        low = dot(vt[:rank], mt_low[:, place])
        result = ((high[:rank] + (high[rank:] + low)) * weight_v).T
        for i in range(2):
            for c in range(2):
                at = (2 * i + c) * own
                mp[to, 2 * slot + i, c] = result[at : at + own]

    def hand_over(k, slot, to):
        at = pl.ds(2 * slot, 2)
        return send(
            mp.at[to, at, 1 - core], first.at[to, at], ref["cs"].at[k, slot], ref["cr"].at[k, slot], pos.partner()
        )

    over = []

    def hand_on(k, slot, to, copy):
        copy.wait_recv()
        at = pl.ds(2 * slot, 2)
        if k == 0:
            second[slab, at] = mp[slab, at, core] + first[slab, at]
            return
        half[to, at] = mp[to, at, core] + first[to, at]
        over.append(
            send(half.at[to, at], second.at[slab, at], ref["ss"].at[k - 1, slot], ref["sr"].at[k - 1, slot], (to, brick))
        )

    waiting = []
    for k in list(range(1, slabs)) + [0]:
        to = lax.rem(slab + k, slabs)
        for slot in range(slots):
            project(to, slot)
            copy = hand_over(k, slot, to)
            if len(waiting) >= 1:
                hand_on(*waiting.pop(0))
            waiting.append((k, slot, to, copy))

    transport_sum.finish()
    packed = ref["to"][...].reshape(3 * rank, rank)
    trans = ref["trans"]
    for d in range(3):
        block = packed[d * rank : (d + 1) * rank]
        flipped = block.T
        diagonal = jnp.where(row == column, vectors[d + 5 : d + 6], 0.0)
        trans[d * rank : (d + 1) * rank] = jnp.where(row <= column, block, flipped)
        trans[(d + 3) * rank : (d + 4) * rank] = jnp.where(
            row > column, block, jnp.where(row < column, flipped, diagonal)
        )
    for copy in waiting:
        hand_on(*copy)
    for copy in halos:
        copy.wait_recv()
    field = k_ref[...]
    after_a = jnp.concatenate([field[1:], halo_a[1:2]], axis=0)
    before_a = jnp.concatenate([halo_a[0:1], field[:-1]], axis=0)
    after_b = jnp.concatenate([field[:, 1:], halo_b[1].reshape(cells_x, 1, cells_z, rank)], axis=1)
    before_b = jnp.concatenate([halo_b[0].reshape(cells_x, 1, cells_z, rank), field[:, :-1]], axis=1)

    def next_third(flat):
        count = flat.shape[0]
        index = lax.broadcasted_iota(jnp.int32, flat.shape, 0)
        return jnp.where(
            lax.rem(index, cells_z) == cells_z - 1,
            pltpu.roll(flat, cells_z - 1, 0),
            pltpu.roll(flat, count - 1, 0),
        )

    def last_third(flat):
        count = flat.shape[0]
        index = lax.broadcasted_iota(jnp.int32, flat.shape, 0)
        return jnp.where(
            lax.rem(index, cells_z) == 0,
            pltpu.roll(flat, count - cells_z + 1, 0),
            pltpu.roll(flat, 1, 0),
        )

    fields = [
        (after_a.reshape(own, rank) - own_k) * lengths[0],
        (after_b.reshape(own, rank) - own_k) * lengths[1],
        (next_third(own_k) - own_k) * lengths[2],
        (own_k - before_a.reshape(own, rank)) * lengths[0],
        (own_k - before_b.reshape(own, rank)) * lengths[1],
        (own_k - last_third(own_k)) * lengths[2],
    ]
    flux = dot3(jnp.concatenate(fields, axis=1), trans[...])
    kept = own_k - time_step * flux - COLLIDE * own_k

    for copy in over:
        copy.wait_recv()
    total = second[0]
    for k in range(1, slabs):
        total = total + second[k]
    quarter = ref["quarter"]
    quarter[...] = total
    copies = []
    for k in range(1, layers):
        to = lax.rem(layer + k, layers)
        copies.append(
            send(quarter.at[to], third.at[layer], ref["zs"].at[k - 1], ref["zr"].at[k - 1], pos.across(k))
        )
    third[layer] = quarter[layer]
    for copy in copies:
        copy.wait_recv()
    mproj = third[0]
    for k in range(1, layers):
        mproj = mproj + third[k]
    advanced = kept + COLLIDE * mproj

    adv = ref["adv"]
    adv[slab, brick] = advanced.reshape(cells_x, cells_y, cells_z, rank)
    here = adv.at[slab, brick]

    def to_slabs(block, j):
        return [
            send(block, block, ref["bs"].at[k - 1, j], ref["br"].at[k - 1, j], pos.slab_at(k)[1])
            for k in range(1, slabs)
        ]

    along = [
        send(here, here, ref["as"].at[k - 1], ref["ar"].at[k - 1], pos.across(k)) for k in range(1, layers)
    ]
    crossing = [to_slabs(here, 0)]
    last = [send(here, here, ref["ds"].at[0, 0], ref["dr"].at[0, 0], pos.partner())]
    raw_sum = Sum(send, pos, ref["rx"], ref["r1"], ref["r2"], ref["ro"], [ref[f"rsem{i}"] for i in range(6)])
    ref["rx"][...] = dot3(advanced.T, mproj).reshape(members, rank // members, rank)
    for j in range(1, layers):
        along[j - 1].wait_recv()
        block = adv.at[slab, 2 * lax.rem(layer + layers - j, layers) + core]
        crossing.append(to_slabs(block, j))
        last.append(send(block, block, ref["ds"].at[0, j], ref["dr"].at[0, j], pos.partner()))
    raw_sum.scatter()
    for j in range(layers):
        for k in range(1, slabs):
            crossing[j][k - 1].wait_recv()
            block = adv.at[lax.rem(slab + slabs - k, slabs), 2 * lax.rem(layer + layers - j, layers) + core]
            last.append(send(block, block, ref["ds"].at[k, j], ref["dr"].at[k, j], pos.partner()))
    raw_sum.cross()
    for copy in last:
        copy.wait_recv()
    raw_sum.collect()

    at, ahl = ref["at"], ref["ahl"]
    d_high, d_low = ref["d_high"], ref["d_low"]
    plane = cells // slabs
    for s in range(slabs):
        block = adv[s]
        flat = block.reshape(plane, rank)
        span = slice(s * plane, (s + 1) * plane)
        high, low = halves(flat)
        ahl[span, :rank] = high
        ahl[span, rank:] = low
        high, low = halves(flat.T)
        at[:rank, span] = high
        at[rank:, span] = low
        following = adv[(s + 1) % slabs]
        up_a = jnp.concatenate([block[:, 1:], following[:, :1]], axis=1)
        wrapped = jnp.concatenate([block[1:, :, :1], block[:1, :, :1]], axis=0)
        up_b = jnp.concatenate([block[:, :, 1:], wrapped], axis=2)
        ups = [up_a.reshape(plane, rank), up_b.reshape(plane, rank), next_third(flat)]
        for d in range(3):
            high, low = halves(ups[d] - flat)
            d_high[span, d * rank : (d + 1) * rank] = high
            d_low[span, d * rank : (d + 1) * rank] = low
    both = dot(at[:rank], ahl[...])
    mixed = both[:, rank:]
    gram = (both[:, :rank] + (mixed + mixed.T)) * weight_x
    factor, inverse = factor_steps(ref["work"], gram)

    both = dot(at[...], d_high[...])
    slopes = both[:rank] + (both[rank:] + dot(at[:rank], d_low[...]))
    slopes = [slopes[:, d * rank : (d + 1) * rank] * (lengths[d] * weight_x) for d in range(3)]
    raw_sum.finish()
    raw = ref["ro"][...].reshape(rank, rank) * weight_x
    source = time_step * dot6(
        jnp.concatenate(slopes + [-item.T for item in slopes], axis=1), trans[...]
    ) - COLLIDE * raw

    place = 2 * own
    scaled = ahl[...]
    top = dot(mt_high[...], scaled)
    low = dot(mt_low[...], ahl[:, :rank])
    back_raw = (top[:, :rank] + (top[:, rank:] + low)) * weight_x

    turned = inverse.T
    middle = (1.0 + COLLIDE) * factor + dot6(source.T, turned)
    moved = dot6(inverse, jnp.concatenate(slopes, axis=1))
    plus = dot6(jnp.concatenate([moved[:, d * rank : (d + 1) * rank] for d in range(3)], axis=0), turned)
    plus = [plus[d * rank : (d + 1) * rank] for d in range(3)]
    sides = jnp.concatenate(plus + [item.T for item in plus], axis=1)
    lnew = ref["lnew"]
    chunk = math.gcd(nodes, 256)
    for at_row in range(0, nodes, chunk):
        span = slice(at_row, at_row + chunk)
        lnow = dot3(v_ref[span, :], middle)
        sliding = dot3(lnow, sides)
        part = node_velocity(base + at_row + lax.broadcasted_iota(jnp.int32, (chunk, rank), 0))
        slide = jnp.zeros((chunk, rank), F32)
        for d in range(3):
            slide = slide + jnp.maximum(part[d], 0.0) * sliding[:, d * rank : (d + 1) * rank]
            slide = slide - jnp.minimum(part[d], 0.0) * sliding[:, (d + 3) * rank : (d + 4) * rank]
        mback = dot3(back_raw[span], turned)
        lnew[span, :] = lnow + time_step * slide + COLLIDE * (mback - lnow)

    new = lnew[...]
    high, low = halves(new)
    rest = (new - high.astype(F32) - low.astype(F32)).astype(BF16)
    new_t = new.T
    high_t, low_t = halves(new_t)
    both = dot(high_t, jnp.concatenate([high, low, rest], axis=1))
    mixed = both[:, rank : 2 * rank] + (both[:, 2 * rank :] + 0.5 * dot(low_t, low))
    gram_v = (both[:, :rank] + (mixed + mixed.T)) * weight_v
    ref["gx"][...] = gram_v.reshape(members, rank // members, rank)
    gram_sum = Sum(send, pos, ref["gx"], ref["g1"], ref["g2"], ref["go"], [ref[f"gsem{i}"] for i in range(6)])
    gram_sum.scatter()
    ref["basis_x"][...] = dot3(advanced, turned).reshape(cells_x, cells_y, cells_z, rank)
    gram_sum.cross()
    gram_sum.collect()
    gram_sum.finish()
    coupling, inverse_v = factor_steps(ref["work"], ref["go"][...].reshape(rank, rank))
    ref["coupling"][...] = coupling
    ref["basis_v"][...] = dot3(lnew[...], inverse_v.T)
    for copy in started:
        copy.wait_send()


def local(k_coeffs, v_basis):
    cells_x, cells_y, cells_z, rank = k_coeffs.shape
    slabs = lax.axis_size("slab")
    layers = lax.axis_size("brick") // 2
    members = 2 * slabs
    own = cells_x * cells_y * cells_z
    nodes = v_basis.shape[0]
    cells = own * members * layers
    share = 3 * rank // members
    part = rank // members
    pair = 2 * own
    names = ["k", "v", "basis_x", "coupling", "basis_v"]
    scratch = []

    def buffer(name, shape, dtype=F32):
        names.append(name)
        scratch.append(pltpu.VMEM(shape, dtype))

    def semaphores(name, *shape):
        names.append(name)
        scratch.append(pltpu.SemaphoreType.DMA(shape))

    def reduction(name, rows):
        buffer(name + "x", (members, rows, rank))
        buffer(name + "1", (members - 1, rows, rank))
        buffer(name + "2", (layers, rows, rank))
        buffer(name + "o", (members, rows, rank))
        for i, count in enumerate([members, members, layers, layers, members, members]):
            semaphores(name + "sem" + str(i), count - 1)

    buffer("vec_l", (layers, 8, rank))
    buffer("vec_m", (members, 8, rank))
    buffer("halo_a", (2, cells_y, cells_z, rank))
    buffer("halo_b", (2, cells_x, cells_z, rank))
    buffer("vt", (2 * rank, nodes), BF16)
    buffer("kpad", (pair, rank))
    buffer("par", (members, layers, 8, pair))
    buffer("mt_high", (nodes, cells), BF16)
    buffer("mt_low", (nodes, cells), BF16)
    buffer("mp", (slabs, layers, 2, own, rank))
    buffer("first", (slabs, layers, own, rank))
    buffer("half", (slabs, layers, own, rank))
    buffer("second", (slabs, layers, own, rank))
    buffer("quarter", (layers, own, rank))
    buffer("third", (layers, own, rank))
    buffer("trans", (6 * rank, rank))
    buffer("adv", (slabs, 2 * layers, cells_x, cells_y, cells_z, rank))
    buffer("at", (2 * rank, cells), BF16)
    buffer("ahl", (cells, 2 * rank), BF16)
    buffer("d_high", (cells, 3 * rank), BF16)
    buffer("d_low", (cells, 3 * rank), BF16)
    buffer("work", (rank, 2 * rank))
    buffer("lnew", (nodes, rank))
    reduction("t", share)
    reduction("r", part)
    reduction("g", part)
    for name in ("vl", "pl", "z", "a"):
        semaphores(name + "s", layers - 1)
        semaphores(name + "r", layers - 1)
    for name in ("vm", "pm"):
        semaphores(name + "s", members - 1)
        semaphores(name + "r", members - 1)
    semaphores("hs", 4)
    semaphores("hr", 4)
    for name, shape in (
        ("c", (slabs, layers // 2)),
        ("s", (slabs - 1, layers // 2)),
        ("b", (slabs - 1, layers)),
        ("d", (slabs, layers)),
    ):
        semaphores(name + "s", *shape)
        semaphores(name + "r", *shape)
    return pl.pallas_call(
        functools.partial(step_kernel, tuple(names), slabs, layers),
        out_shape=(
            jax.ShapeDtypeStruct(k_coeffs.shape, F32),
            jax.ShapeDtypeStruct((rank, rank), F32),
            jax.ShapeDtypeStruct(v_basis.shape, F32),
        ),
        in_specs=[VM, VM],
        out_specs=(VM, VM, VM),
        scratch_shapes=scratch,
        compiler_params=pltpu.CompilerParams(
            collective_id=1, has_side_effects=True, vmem_limit_bytes=60 * 2**20
        ),
    )(k_coeffs, v_basis)


def solution(mesh):
    return jax.shard_map(
        local,
        mesh=mesh,
        in_specs=(P("slab", "brick", None, None), P(("slab", "brick"), None)),
        out_specs=(P("slab", "brick", None, None), P(), P(("slab", "brick"), None)),
        check_vma=False,
    )
```

time: 143 us -> 90.9 us (0.64)
  Pallas kernels: 106 us -> 86.1 us
  matrix products: 19.2 us -> 0 us
  other arithmetic: 7.53 us -> 0 us
  local copies, waits for them, and re-layouts: 8.52 us -> 3.91 us
    pallas_call x8 -> x1, Pallas kernels: 106 us -> 86.1 us  [local(): pl.pallas_call(functools.partial(step_kernel, tuple(names), slabs, layers...]
    dot_general x20 -> x0, matrix products: 19.2 us -> none  [the longest x6 4.92 us: local(): jnp.dot(item.reshape(cells, rank), transport[k * rank:(k + 1) * rank], pr...]
    concatenate x7 -> x0, other arithmetic: 4.15 us -> none  [the longest x1 2.43 us: local(): jnp.concatenate([mproj_part, transport_part.reshape(6 * rank, rank)])]
    transpose x2 -> x0, local copies, waits for them, and re-layouts: 2.14 us -> none  [the longest x1 1.31 us: local(): mproj_part = project(rows.T, velocity_rows, v_basis, weight_v)]
    slice x15 -> x0, local copies, waits for them, and re-layouts: 1.8 us -> none  [the longest x1 1.04 us: local(): mproj = summed[:cells]]
    another operation x1 -> x0, other arithmetic: 1.58 us -> none  [local(): slopes_raw = jnp.stack([raw[d] * (lengths[d] * weight_x) for d in range(3)])]
    unnamed x17 -> x5, local copies, waits for them, and re-layouts: 2.82 us -> 3.91 us
where the time goes in v1:
time: 90.9 us; the launch traced here: 90.6 us
  Pallas kernels  86.1 us (95%)
  local copies, waits for them, and re-layouts  3.91 us (4%)
    pallas_call x1, Pallas kernels, local(): pl.pallas_call(functools.partial(step_kernel, tuple(names), slabs, layers...  86.1 us
    unnamed x5, local copies, waits for them, and re-layouts  3.91 us

profile of v1, /device:TPU:0, one launch (start us, length us, event | category | flops | bytes accessed | tf_op | source)
XLA Modules:
  0.0 90.6 jit_solution(140493240150280006)
XLA Ops:
  0.6 86.1 %shard_map.49 = (f32[2,2,16,128]{3,2,1,0:T(8,128)}, f32[128,128]{1,0:T(8,128)}, f32[1024,128]{1,0:T(8,128)}) custom-call(f32[2,2,16,128]{3,2,1,0:T(8,128)} %refs_0_.1, f32[1024,128]{1,0:T(8,128)} %refs_1_.1), custom_call_target="tpu_custom_call" | custom-call | tf_op jit(solution)/shard_map/pallas_call | solution.py:632
  86.7 0.0 copy-start
  86.7 1.4 %copy.8 = f32[2,2,16,128]{3,2,1,0:T(8,128)} copy(f32[2,2,16,128]{3,2,1,0:T(8,128)} %get-tuple-element.6) | data formatting | bytes 65536
  88.1 0.0 copy-done
  88.1 0.6 copy.9
  88.8 1.9 %copy.10 = f32[1024,128]{1,0:T(8,128)} copy(f32[1024,128]{1,0:T(8,128)} %get-tuple-element.8) | data formatting | bytes 1048576
Async XLA Ops:
  86.7 1.4 %copy-start = (f32[128,128]{1,0:T(8,128)S(1)}, f32[128,128]{1,0:T(8,128)}, u32[]{:S(2)}) copy-start(f32[128,128]{1,0:T(8,128)} %get-tuple-element.7) | copy-start | bytes 196612

commit v2 on v1

--- a/solution.py
+++ b/solution.py
@@ -18,6 +18,7 @@
 PRECISE = lax.Precision.HIGHEST
 MESH = pl.DeviceIdType.MESH
 VM = pl.BlockSpec(memory_space=pltpu.VMEM)
+ANY = pl.BlockSpec(memory_space=pl.ANY)
 F32 = jnp.float32
 BF16 = jnp.bfloat16
 BITS = NVX.bit_length() - 1
@@ -122,6 +123,14 @@
 
     def across(self, k):
         return (self.slab, 2 * lax.rem(self.layer + k, self.layers) + self.core)
+
+    def others(self):
+        bricks = 2 * self.layers
+        count = self.slabs * bricks
+        at = self.slab * bricks + self.brick
+        for k in range(1, count):
+            to = lax.rem(at + k, count)
+            yield k - 1, (lax.div(to, bricks), lax.rem(to, bricks))
 
     def partner(self):
         return (self.slab, 2 * self.layer + 1 - self.core)
@@ -198,9 +207,7 @@
         return copy
 
     barrier = pltpu.get_barrier_semaphore()
-    peers = [pos.member(k)[1] for k in range(1, members)]
-    peers += [pos.across(k) for k in range(1, layers)]
-    peers += [pos.brick_at(1), pos.brick_at(-1)]
+    peers = [device for _, device in pos.others()]
     for peer in peers:
         pl.semaphore_signal(barrier, inc=1, device_id=peer, device_id_type=MESH)
 
@@ -221,21 +228,8 @@
     squares = dot(upward.astype(BF16), jnp.concatenate(halves(values * values), axis=1))
     partial = sums[:, :rank] + (sums[:, rank : 2 * rank] + sums[:, 2 * rank :])
     partial = (partial + (squares[:, :rank] + squares[:, rank:])) * weight_v
-    vec_l, vec_m = ref["vec_l"], ref["vec_m"]
-    vec_l[layer] = partial
-
-    pl.semaphore_wait(barrier, len(peers))
-    mine = vec_l.at[layer]
-    copies = [
-        send(mine, mine, ref["vls"].at[k - 1], ref["vlr"].at[k - 1], pos.across(k)) for k in range(1, layers)
-    ]
-    halo_a, halo_b = ref["halo_a"], ref["halo_b"]
-    halos = [
-        send(k_ref.at[cells_x - 1], halo_a.at[0], ref["hs"].at[0], ref["hr"].at[0], pos.slab_at(1)[1]),
-        send(k_ref.at[0], halo_a.at[1], ref["hs"].at[1], ref["hr"].at[1], pos.slab_at(slabs - 1)[1]),
-        send(k_ref.at[:, cells_y - 1], halo_b.at[0], ref["hs"].at[2], ref["hr"].at[2], pos.brick_at(1)),
-        send(k_ref.at[:, 0], halo_b.at[1], ref["hs"].at[3], ref["hr"].at[3], pos.brick_at(-1)),
-    ]
+    vec = ref["vec"]
+    vec[slab, brick] = partial
 
     turned_v = values.T
     vt_high, vt_low = halves(turned_v)
@@ -246,38 +240,44 @@
     row = lax.broadcasted_iota(jnp.int32, (rank, rank), 0)
     column = lax.broadcasted_iota(jnp.int32, (rank, rank), 1)
     packed = []
-    for d in range(3):
+
+    def pack(d):
         sides = []
         for side in (jnp.maximum(velocity[d][:1], 0.0), jnp.minimum(velocity[d][:1], 0.0)):
             high, low = halves(turned_v * (side * weight_v))
             both = dot(high, v_both)
             sides.append(both[:, :rank] + (both[:, rank:] + dot(low, v_high)))
         packed.append(jnp.where(row > column, sides[0], sides[1]))
+
+    pack(0)
+    pack(1)
+    pl.semaphore_wait(barrier, len(peers))
+    mine = vec.at[slab, brick]
+    copies = [send(mine, mine, ref["vs"].at[i], ref["vr"].at[i], device) for i, device in pos.others()]
+    halo_a, halo_b = ref["halo_a"], ref["halo_b"]
+    halos = [
+        send(k_ref.at[cells_x - 1], halo_a.at[0], ref["hs"].at[0], ref["hr"].at[0], pos.slab_at(1)[1]),
+        send(k_ref.at[0], halo_a.at[1], ref["hs"].at[1], ref["hr"].at[1], pos.slab_at(slabs - 1)[1]),
+        send(k_ref.at[:, cells_y - 1], halo_b.at[0], ref["hs"].at[2], ref["hr"].at[2], pos.brick_at(1)),
+        send(k_ref.at[:, 0], halo_b.at[1], ref["hs"].at[3], ref["hr"].at[3], pos.brick_at(-1)),
+    ]
+
+    pack(2)
     share = 3 * rank // members
     ref["tx"][...] = jnp.concatenate(packed, axis=0).reshape(members, share, rank)
     transport_sum = Sum(send, pos, ref["tx"], ref["t1"], ref["t2"], ref["to"], [ref[f"tsem{i}"] for i in range(6)])
+    transport_sum.scatter()
 
     for copy in copies:
         copy.wait_recv()
-    total = vec_l[0]
-    for k in range(1, layers):
-        total = total + vec_l[k]
-    vec_m[me] = total
-    mine = vec_m.at[me]
-    copies = [
-        send(mine, mine, ref["vms"].at[k - 1], ref["vmr"].at[k - 1], pos.member(k)[1]) for k in range(1, members)
-    ]
-    transport_sum.scatter()
+    vectors = vec[0, 0]
+    for k in range(1, slabs * bricks):
+        vectors = vectors + vec[k // bricks, k % bricks]
+
     own_k = k_ref[...].reshape(own, rank)
     kpad = ref["kpad"]
     kpad[...] = jnp.zeros_like(kpad)
     kpad[pl.ds(pl.multiple_of(core * own, 8), own), :] = own_k
-    for copy in copies:
-        copy.wait_recv()
-    vectors = vec_m[0]
-    for k in range(1, members):
-        vectors = vectors + vec_m[k]
-
     moments = lax.dot_general(
         vectors, kpad[...], (((1,), (1,)), ((), ())), precision=PRECISE, preferred_element_type=F32
     )
@@ -297,19 +297,11 @@
     par = ref["par"]
     par[me, layer] = jnp.where(inside, state, 0.0)
     mine = par.at[me, layer]
-    copies = [
-        send(mine, mine, ref["pls"].at[k - 1], ref["plr"].at[k - 1], pos.across(k)) for k in range(1, layers)
-    ]
+    copies = [send(mine, mine, ref["ps"].at[i], ref["pr"].at[i], device) for i, device in pos.others()]
     transport_sum.cross()
     for copy in copies:
         copy.wait_recv()
-    mine = par.at[me]
-    copies = [
-        send(mine, mine, ref["pms"].at[k - 1], ref["pmr"].at[k - 1], pos.member(k)[1]) for k in range(1, members)
-    ]
     transport_sum.collect()
-    for copy in copies:
-        copy.wait_recv()
 
     mt_high, mt_low = ref["mt_high"], ref["mt_low"]
     mp, first, half, second, third = ref["mp"], ref["first"], ref["half"], ref["second"], ref["third"]
@@ -462,16 +454,14 @@
         block = adv.at[slab, 2 * lax.rem(layer + layers - j, layers) + core]
         crossing.append(to_slabs(block, j))
         last.append(send(block, block, ref["ds"].at[0, j], ref["dr"].at[0, j], pos.partner()))
-    raw_sum.scatter()
     for j in range(layers):
         for k in range(1, slabs):
             crossing[j][k - 1].wait_recv()
             block = adv.at[lax.rem(slab + slabs - k, slabs), 2 * lax.rem(layer + layers - j, layers) + core]
             last.append(send(block, block, ref["ds"].at[k, j], ref["dr"].at[k, j], pos.partner()))
-    raw_sum.cross()
+    raw_sum.scatter()
     for copy in last:
         copy.wait_recv()
-    raw_sum.collect()
 
     at, ahl = ref["at"], ref["ahl"]
     d_high, d_low = ref["d_high"], ref["d_low"]
@@ -495,6 +485,7 @@
             high, low = halves(ups[d] - flat)
             d_high[span, d * rank : (d + 1) * rank] = high
             d_low[span, d * rank : (d + 1) * rank] = low
+    raw_sum.cross()
     both = dot(at[:rank], ahl[...])
     mixed = both[:, rank:]
     gram = (both[:, :rank] + (mixed + mixed.T)) * weight_x
@@ -503,6 +494,7 @@
     both = dot(at[...], d_high[...])
     slopes = both[:rank] + (both[rank:] + dot(at[:rank], d_low[...]))
     slopes = [slopes[:, d * rank : (d + 1) * rank] * (lengths[d] * weight_x) for d in range(3)]
+    raw_sum.collect()
     raw_sum.finish()
     raw = ref["ro"][...].reshape(rank, rank) * weight_x
     source = time_step * dot6(
@@ -543,18 +535,69 @@
     both = dot(high_t, jnp.concatenate([high, low, rest], axis=1))
     mixed = both[:, rank : 2 * rank] + (both[:, 2 * rank :] + 0.5 * dot(low_t, low))
     gram_v = (both[:, :rank] + (mixed + mixed.T)) * weight_v
-    ref["gx"][...] = gram_v.reshape(members, rank // members, rank)
-    gram_sum = Sum(send, pos, ref["gx"], ref["g1"], ref["g2"], ref["go"], [ref[f"gsem{i}"] for i in range(6)])
-    gram_sum.scatter()
-    ref["basis_x"][...] = dot3(advanced, turned).reshape(cells_x, cells_y, cells_z, rank)
-    gram_sum.cross()
-    gram_sum.collect()
-    gram_sum.finish()
-    coupling, inverse_v = factor_steps(ref["work"], ref["go"][...].reshape(rank, rank))
-    ref["coupling"][...] = coupling
-    ref["basis_v"][...] = dot3(lnew[...], inverse_v.T)
+    half_rank = rank // 2
+    lanes = lax.broadcasted_iota(jnp.int32, (half_rank // 2, rank), 1)
+    corner = jnp.where(
+        lanes < half_rank,
+        pltpu.roll(gram_v[half_rank : half_rank + half_rank // 2], half_rank, 1),
+        gram_v[half_rank + half_rank // 2 :],
+    )
+    gx, g1, g2, g3, go = ref["gx"], ref["g1"], ref["g2"], ref["g3"], ref["go"]
+    gx[...] = jnp.concatenate([gram_v[:half_rank], corner], axis=0).reshape(gx.shape)
+    copy = send(gx.at[1 - core], g1, ref["gcs"].at[0], ref["gcr"].at[0], pos.partner())
+    copy.wait_recv()
+    g2[slab] = gx[core] + g1[...]
+    mine = g2.at[slab]
+    copies = [
+        send(mine, mine, ref["gss"].at[k - 1], ref["gsr"].at[k - 1], pos.slab_at(k)[1]) for k in range(1, slabs)
+    ]
+    ref["basis_x"][...] = dot3(advanced, turned)
+    for copy in copies:
+        copy.wait_recv()
+    total = g2[0]
+    for k in range(1, slabs):
+        total = total + g2[k]
+    g3[layer] = total
+    mine = g3.at[layer]
+    copies = [
+        send(mine, mine, ref["gls"].at[k - 1], ref["glr"].at[k - 1], pos.across(k)) for k in range(1, layers)
+    ]
+    for copy in copies:
+        copy.wait_recv()
+    total = g3[0]
+    for k in range(1, layers):
+        total = total + g3[k]
+    go[core] = total
+    mine = go.at[core]
+    send(mine, mine, ref["gcs"].at[1], ref["gcr"].at[1], pos.partner()).wait_recv()
+    whole = go[...].reshape(half_rank + half_rank // 2, rank)
+    corner = whole[half_rank:]
+    gram_ref = ref["gram"]
+    gram_ref[:half_rank] = whole[:half_rank]
+    gram_ref[half_rank : half_rank + half_rank // 2] = pltpu.roll(corner, half_rank, 1)
+    gram_ref[half_rank + half_rank // 2 :] = corner
     for copy in started:
         copy.wait_send()
+
+
+def finish_kernel(gram, lnew, field, basis_x, coupling, basis_v, work, factor_buffer, out, sems):
+    give = pltpu.make_async_copy(field, basis_x, sems.at[0])
+    give.start()
+    factor, inverse = factor_steps(work, gram[...])
+    factor_buffer[...] = factor
+    copies = [give, pltpu.make_async_copy(factor_buffer, coupling, sems.at[1])]
+    copies[1].start()
+    turned = inverse.T
+    nodes = lnew.shape[0]
+    count = sems.shape[0] - 2
+    chunk = nodes // count
+    for i in range(count):
+        span = pl.ds(i * chunk, chunk)
+        out[span, :] = dot3(lnew[span, :], turned)
+        copies.append(pltpu.make_async_copy(out.at[span], basis_v.at[span], sems.at[2 + i]))
+        copies[-1].start()
+    for copy in copies:
+        copy.wait()
 
 
 def local(k_coeffs, v_basis):
@@ -568,11 +611,15 @@
     share = 3 * rank // members
     part = rank // members
     pair = 2 * own
-    names = ["k", "v", "basis_x", "coupling", "basis_v"]
+    devices = members * layers
+    names = ["k", "v", "basis_x", "gram", "lnew"]
     scratch = []
+
+    used = [0]
 
     def buffer(name, shape, dtype=F32):
         names.append(name)
+        used[0] += math.prod(shape) * jnp.dtype(dtype).itemsize
         scratch.append(pltpu.VMEM(shape, dtype))
 
     def semaphores(name, *shape):
@@ -587,8 +634,7 @@
         for i, count in enumerate([members, members, layers, layers, members, members]):
             semaphores(name + "sem" + str(i), count - 1)
 
-    buffer("vec_l", (layers, 8, rank))
-    buffer("vec_m", (members, 8, rank))
+    buffer("vec", (slabs, 2 * layers, 8, rank))
     buffer("halo_a", (2, cells_y, cells_z, rank))
     buffer("halo_b", (2, cells_x, cells_z, rank))
     buffer("vt", (2 * rank, nodes), BF16)
@@ -609,16 +655,20 @@
     buffer("d_high", (cells, 3 * rank), BF16)
     buffer("d_low", (cells, 3 * rank), BF16)
     buffer("work", (rank, 2 * rank))
-    buffer("lnew", (nodes, rank))
     reduction("t", share)
     reduction("r", part)
-    reduction("g", part)
-    for name in ("vl", "pl", "z", "a"):
+    packed = 3 * rank // 8
+    buffer("gx", (2, packed, rank))
+    buffer("g1", (packed, rank))
+    buffer("g2", (slabs, packed, rank))
+    buffer("g3", (layers, packed, rank))
+    buffer("go", (2, packed, rank))
+    for name, count in (("gc", 2), ("gs", slabs - 1), ("v", devices - 1), ("p", devices - 1)):
+        semaphores(name + "s", count)
+        semaphores(name + "r", count)
+    for name in ("gl", "z", "a"):
         semaphores(name + "s", layers - 1)
         semaphores(name + "r", layers - 1)
-    for name in ("vm", "pm"):
-        semaphores(name + "s", members - 1)
-        semaphores(name + "r", members - 1)
     semaphores("hs", 4)
     semaphores("hr", 4)
     for name, shape in (
@@ -629,10 +679,10 @@
     ):
         semaphores(name + "s", *shape)
         semaphores(name + "r", *shape)
-    return pl.pallas_call(
+    basis_x, gram, lnew = pl.pallas_call(
         functools.partial(step_kernel, tuple(names), slabs, layers),
         out_shape=(
-            jax.ShapeDtypeStruct(k_coeffs.shape, F32),
+            jax.ShapeDtypeStruct((own, rank), F32),
             jax.ShapeDtypeStruct((rank, rank), F32),
             jax.ShapeDtypeStruct(v_basis.shape, F32),
         ),
@@ -640,9 +690,28 @@
         out_specs=(VM, VM, VM),
         scratch_shapes=scratch,
         compiler_params=pltpu.CompilerParams(
-            collective_id=1, has_side_effects=True, vmem_limit_bytes=60 * 2**20
+            collective_id=1, has_side_effects=True, vmem_limit_bytes=min(60 * 2**20, used[0] + 10 * 2**20)
         ),
     )(k_coeffs, v_basis)
+    chunks = 4
+    basis_x, coupling, basis_v = pl.pallas_call(
+        finish_kernel,
+        out_shape=(
+            jax.ShapeDtypeStruct((own, rank), F32),
+            jax.ShapeDtypeStruct((rank, rank), F32),
+            jax.ShapeDtypeStruct(v_basis.shape, F32),
+        ),
+        in_specs=[VM, VM, VM],
+        out_specs=(ANY, ANY, ANY),
+        scratch_shapes=[
+            pltpu.VMEM((rank, 2 * rank), F32),
+            pltpu.VMEM((rank, rank), F32),
+            pltpu.VMEM(v_basis.shape, F32),
+            pltpu.SemaphoreType.DMA((2 + chunks,)),
+        ],
+        compiler_params=pltpu.CompilerParams(vmem_limit_bytes=12 * 2**20),
+    )(gram, lnew, basis_x)
+    return basis_x.reshape(k_coeffs.shape), coupling, basis_v
 
 
 def solution(mesh):

time: 90.9 us -> 86.9 us (0.956)
  Pallas kernels: 86.1 us -> 83.9 us
  local copies, waits for them, and re-layouts: 3.91 us -> 1.79 us
    pallas_call x1, Pallas kernels: 86.1 us -> 75.4 us  [local(): pl.pallas_call(functools.partial(step_kernel, tuple(names), slabs, layers...]
    pallas_call x0 -> x1, Pallas kernels: none -> 8.47 us  [local(): pl.pallas_call(finish_kernel, out_shape=(jax.ShapeDtypeStruct((own, rank)...]
    unnamed x5 -> x4, local copies, waits for them, and re-layouts: 3.91 us -> 1.79 us
where the time goes in v2:
time: 86.9 us; the launch traced here: 86.5 us
  Pallas kernels  83.9 us (97%)
  local copies, waits for them, and re-layouts  1.79 us (2%)
    pallas_call x1, Pallas kernels, local(): pl.pallas_call(functools.partial(step_kernel, tuple(names), slabs, layers...  75.4 us
    pallas_call x1, Pallas kernels, local(): pl.pallas_call(finish_kernel, out_shape=(jax.ShapeDtypeStruct((own, rank)...  8.47 us
    unnamed x4, local copies, waits for them, and re-layouts  1.79 us

profile of v2, /device:TPU:0, one launch (start us, length us, event | category | flops | bytes accessed | tf_op | source)
XLA Modules:
  0.0 86.5 jit_solution(4024595466861094698)
XLA Ops:
  0.6 0.0 copy-start
  0.6 1.0 %copy-done = f32[1024,128]{1,0:T(8,128)S(1)} copy-done((f32[1024,128]{1,0:T(8,128)S(1)}, f32[1024,128]{1,0:T(8,128)}, u32[]{:S(2)}) %copy-start) | copy-done | bytes 524312
  1.7 0.0 copy-start.1
  1.7 0.8 copy-done.1
  2.4 75.4 %shard_map.49 = (f32[64,128]{1,0:T(8,128)S(1)}, f32[128,128]{1,0:T(8,128)S(1)}, f32[1024,128]{1,0:T(8,128)S(1)}) custom-call(f32[2,2,16,128]{3,2,1,0:T(8,128)S(1)} %copy-done.1, f32[1024,128]{1,0:T(8,128)S(1)} %copy-done), custom_call_target="tpu_custom_call" | custom-call | tf_op jit(solution)/shard_map/pallas_call | solution.py:682
  77.9 8.5 %shard_map.50 = (f32[64,128]{1,0:T(8,128)}, f32[128,128]{1,0:T(8,128)}, f32[1024,128]{1,0:T(8,128)}) custom-call(f32[128,128]{1,0:T(8,128)S(1)} %get-tuple-element.9.gram, f32[1024,128]{1,0:T(8,128)S(1)} %get-tuple-element.10.lnew, f32[64,128]{1,0:T(8,128)S(1)} %get-tuple-element.11.field), custom_call_target="tpu_custom_call" | custom-call | tf_op jit(solution)/shard_map/pallas_call | solution.py:697
Async XLA Ops:
  0.6 1.0 %copy-start = (f32[1024,128]{1,0:T(8,128)S(1)}, f32[1024,128]{1,0:T(8,128)}, u32[]{:S(2)}) copy-start(f32[1024,128]{1,0:T(8,128)} %refs_1_.1) | copy-start | bytes 1572868
  1.7 0.8 copy-start.1

commit v3 on v2

--- a/solution.py
+++ b/solution.py
@@ -18,7 +18,7 @@
 PRECISE = lax.Precision.HIGHEST
 MESH = pl.DeviceIdType.MESH
 VM = pl.BlockSpec(memory_space=pltpu.VMEM)
-ANY = pl.BlockSpec(memory_space=pl.ANY)
+HBM = pl.BlockSpec(memory_space=pltpu.HBM)
 F32 = jnp.float32
 BF16 = jnp.bfloat16
 BITS = NVX.bit_length() - 1
@@ -41,7 +41,15 @@
 
 
 def dot3(left, right):
-    return dot_split(*halves(left), right)
+    depth, width = right.shape
+    high, low = halves(left)
+    if depth != 128:
+        return dot_split(high, low, right)
+    right_high, right_low = halves(right)
+    top = jnp.concatenate([right_high, right_low], axis=1)
+    under = jnp.concatenate([right_high, jnp.zeros_like(right_low)], axis=1)
+    both = dot(jnp.concatenate([high, low], axis=1), jnp.concatenate([top, under], axis=0))
+    return both[:, :width] + both[:, width:]
 
 
 def dot6(left, right):
@@ -121,6 +129,18 @@
         to = lax.rem(self.me + k, self.members)
         return to, (lax.div(to, 2), 2 * self.layer + lax.rem(to, 2))
 
+    def mate(self, k):
+        if self.layers != 4:
+            return lax.rem(self.layer + k, self.layers)
+        if k == 1:
+            return self.layer + 1 - 2 * lax.rem(self.layer, 2)
+        return lax.rem(self.layer + 2, self.layers) if k == 2 else self.layers - 1 - self.layer
+
+    def source(self, k):
+        if k == 0:
+            return self.layer
+        return self.mate(k) if self.layers == 4 else lax.rem(self.layer + self.layers - k, self.layers)
+
     def across(self, k):
         return (self.slab, 2 * lax.rem(self.layer + k, self.layers) + self.core)
 
@@ -146,31 +166,48 @@
 
 def factor_steps(work, matrix):
     size = matrix.shape[0]
-    panel = 8
+    block, panel = 8, 16
     row = lax.broadcasted_iota(jnp.int32, (size, size), 0)
     column = lax.broadcasted_iota(jnp.int32, (size, size), 1)
     work[:, :size] = matrix
     work[:, size:] = jnp.where(row == column, 1.0, 0.0)
-    sub_one = lax.broadcasted_iota(jnp.int32, (panel, size), 0)
+    sub = lax.broadcasted_iota(jnp.int32, (block, size), 0)
+    narrow, wide = (block, size), (block, 2 * size)
     for start in range(0, size, panel):
-        rows = work[start : start + panel, :]
-        columns = [
-            jnp.broadcast_to(rows[:, start + k : start + k + 1], (panel, size))
-            for k in range(panel)
-        ]
-        for k in range(panel):
-            scale = lax.rsqrt(columns[k][k : k + 1, :])
-            ratio = columns[k] * (scale * scale)
-            ratio = jnp.where(sub_one > k, ratio, jnp.where(sub_one == k, 1.0 - scale, 0.0))
-            for m in range(k + 1, panel):
-                columns[m] = columns[m] - ratio * columns[m][k : k + 1, :]
-            rows = rows - jnp.concatenate([ratio, ratio], axis=1) * rows[k : k + 1, :]
-        work[start : start + panel, :] = rows
+        rows = [work[start : start + block, :], work[start + block : start + panel, :]]
+        for b in range(2):
+            at = start + b * block
+            columns = {
+                (r, m): jnp.broadcast_to(rows[r][:, at + m : at + m + 1], narrow)
+                for r in range(b, 2)
+                for m in range(block)
+            }
+            entry = {
+                (i, m): jnp.broadcast_to(columns[b, m][i : i + 1], narrow) for m in range(block) for i in range(m, block)
+            }
+            scales = entry[0, 0]
+            for k in range(block):
+                scale = lax.rsqrt(entry[k, k])
+                invert = scale * scale
+                scales = scale if k == 0 else jnp.where(sub == k, scale, scales)
+                ratios = {r: columns[r, k] * invert for r in range(b, 2)}
+                ratios[b] = jnp.where(sub > k, ratios[b], 0.0)
+                for m in range(k + 1, block):
+                    factor = entry[m, k] * invert
+                    for i in range(m, block):
+                        entry[i, m] = entry[i, m] - entry[i, k] * factor
+                for r in range(b, 2):
+                    for m in range(k + 1, block):
+                        columns[r, m] = columns[r, m] - ratios[r] * entry[m, k]
+                pivot = jnp.broadcast_to(rows[b][k : k + 1], wide)
+                for r in range(b, 2):
+                    rows[r] = rows[r] - jnp.concatenate([ratios[r], ratios[r]], axis=1) * pivot
+            rows[b] = rows[b] * jnp.concatenate([scales, scales], axis=1)
+        both = jnp.concatenate(rows, axis=0)
+        work[start : start + panel, :] = both
         if start + panel < size:
-            tall = rows[:, :size].T[start + panel :, :]
-            work[start + panel :, :] = work[start + panel :, :] - jnp.dot(
-                tall, rows, precision=PRECISE, preferred_element_type=F32
-            )
+            tall = both[:, :size].T[start + panel :, :]
+            work[start + panel :, :] = work[start + panel :, :] - dot6(tall, both)
     factor = jnp.where(column <= row, work[:, :size].T, 0.0)
     inverse = jnp.where(column <= row, work[:, size:], 0.0)
     return factor, inverse
@@ -181,7 +218,13 @@
     pos = Position(slabs, layers)
     core, slab, layer, brick, me = pos.core, pos.slab, pos.layer, pos.brick, pos.me
     members, bricks = pos.members, 2 * layers
-    k_ref, v_ref = ref["k"], ref["v"]
+    k_ref, v_ref = ref["k_here"], ref["v_here"]
+    inputs = [
+        pltpu.make_async_copy(ref["k"], k_ref, ref["insem"].at[0]),
+        pltpu.make_async_copy(ref["v"], v_ref, ref["insem"].at[1]),
+    ]
+    for copy in inputs:
+        copy.start()
     cells_x, cells_y, cells_z, rank = k_ref.shape
     own = cells_x * cells_y * cells_z
     nodes = v_ref.shape[0]
@@ -220,6 +263,8 @@
     for d in range(3):
         weights = jnp.where(sub == d + 1, velocity[d], weights)
         upward = jnp.where(sub == d + 5, jnp.maximum(velocity[d], 0.0), upward)
+    for copy in inputs:
+        copy.wait()
     values = v_ref[...]
     v_high, v_low = halves(values)
     v_rest = (values - v_high.astype(F32) - v_low.astype(F32)).astype(BF16)
@@ -250,7 +295,6 @@
         packed.append(jnp.where(row > column, sides[0], sides[1]))
 
     pack(0)
-    pack(1)
     pl.semaphore_wait(barrier, len(peers))
     mine = vec.at[slab, brick]
     copies = [send(mine, mine, ref["vs"].at[i], ref["vr"].at[i], device) for i, device in pos.others()]
@@ -262,6 +306,7 @@
         send(k_ref.at[:, 0], halo_b.at[1], ref["hs"].at[3], ref["hr"].at[3], pos.brick_at(-1)),
     ]
 
+    pack(1)
     pack(2)
     share = 3 * rank // members
     ref["tx"][...] = jnp.concatenate(packed, axis=0).reshape(members, share, rank)
@@ -298,10 +343,9 @@
     par[me, layer] = jnp.where(inside, state, 0.0)
     mine = par.at[me, layer]
     copies = [send(mine, mine, ref["ps"].at[i], ref["pr"].at[i], device) for i, device in pos.others()]
+    for copy in copies:
+        copy.wait_recv()
     transport_sum.cross()
-    for copy in copies:
-        copy.wait_recv()
-    transport_sum.collect()
 
     mt_high, mt_low = ref["mt_high"], ref["mt_low"]
     mp, first, half, second, third = ref["mp"], ref["first"], ref["half"], ref["second"], ref["third"]
@@ -361,6 +405,10 @@
                 hand_on(*waiting.pop(0))
             waiting.append((k, slot, to, copy))
 
+    transport_sum.collect()
+    for copy in waiting:
+        hand_on(*copy)
+
     transport_sum.finish()
     packed = ref["to"][...].reshape(3 * rank, rank)
     trans = ref["trans"]
@@ -372,8 +420,6 @@
         trans[(d + 3) * rank : (d + 4) * rank] = jnp.where(
             row > column, block, jnp.where(row < column, flipped, diagonal)
         )
-    for copy in waiting:
-        hand_on(*copy)
     for copy in halos:
         copy.wait_recv()
     field = k_ref[...]
@@ -443,23 +489,26 @@
         ]
 
     along = [
-        send(here, here, ref["as"].at[k - 1], ref["ar"].at[k - 1], pos.across(k)) for k in range(1, layers)
+        send(here, here, ref["as"].at[k - 1], ref["ar"].at[k - 1], (slab, 2 * pos.mate(k) + core))
+        for k in range(1, layers)
     ]
     crossing = [to_slabs(here, 0)]
     last = [send(here, here, ref["ds"].at[0, 0], ref["dr"].at[0, 0], pos.partner())]
     raw_sum = Sum(send, pos, ref["rx"], ref["r1"], ref["r2"], ref["ro"], [ref[f"rsem{i}"] for i in range(6)])
     ref["rx"][...] = dot3(advanced.T, mproj).reshape(members, rank // members, rank)
+    raw_sum.scatter()
     for j in range(1, layers):
         along[j - 1].wait_recv()
-        block = adv.at[slab, 2 * lax.rem(layer + layers - j, layers) + core]
+        block = adv.at[slab, 2 * pos.source(j) + core]
         crossing.append(to_slabs(block, j))
         last.append(send(block, block, ref["ds"].at[0, j], ref["dr"].at[0, j], pos.partner()))
+    raw_sum.cross()
     for j in range(layers):
         for k in range(1, slabs):
             crossing[j][k - 1].wait_recv()
-            block = adv.at[lax.rem(slab + slabs - k, slabs), 2 * lax.rem(layer + layers - j, layers) + core]
+            block = adv.at[lax.rem(slab + slabs - k, slabs), 2 * pos.source(j) + core]
             last.append(send(block, block, ref["ds"].at[k, j], ref["dr"].at[k, j], pos.partner()))
-    raw_sum.scatter()
+    raw_sum.collect()
     for copy in last:
         copy.wait_recv()
 
@@ -485,7 +534,6 @@
             high, low = halves(ups[d] - flat)
             d_high[span, d * rank : (d + 1) * rank] = high
             d_low[span, d * rank : (d + 1) * rank] = low
-    raw_sum.cross()
     both = dot(at[:rank], ahl[...])
     mixed = both[:, rank:]
     gram = (both[:, :rank] + (mixed + mixed.T)) * weight_x
@@ -494,7 +542,6 @@
     both = dot(at[...], d_high[...])
     slopes = both[:rank] + (both[rank:] + dot(at[:rank], d_low[...]))
     slopes = [slopes[:, d * rank : (d + 1) * rank] * (lengths[d] * weight_x) for d in range(3)]
-    raw_sum.collect()
     raw_sum.finish()
     raw = ref["ro"][...].reshape(rank, rank) * weight_x
     source = time_step * dot6(
@@ -512,29 +559,32 @@
     moved = dot6(inverse, jnp.concatenate(slopes, axis=1))
     plus = dot6(jnp.concatenate([moved[:, d * rank : (d + 1) * rank] for d in range(3)], axis=0), turned)
     plus = [plus[d * rank : (d + 1) * rank] for d in range(3)]
-    sides = jnp.concatenate(plus + [item.T for item in plus], axis=1)
     lnew = ref["lnew"]
-    chunk = math.gcd(nodes, 256)
+    chunk = math.gcd(nodes, NVX * NVX // 4)
+    gram_v = jnp.zeros((rank, rank), F32)
+    mixed_v = jnp.zeros((rank, rank), F32)
+    back = [-item.T for item in plus]
     for at_row in range(0, nodes, chunk):
         span = slice(at_row, at_row + chunk)
+        node = base + at_row
         lnow = dot3(v_ref[span, :], middle)
-        sliding = dot3(lnow, sides)
-        part = node_velocity(base + at_row + lax.broadcasted_iota(jnp.int32, (chunk, rank), 0))
-        slide = jnp.zeros((chunk, rank), F32)
-        for d in range(3):
-            slide = slide + jnp.maximum(part[d], 0.0) * sliding[:, d * rank : (d + 1) * rank]
-            slide = slide - jnp.minimum(part[d], 0.0) * sliding[:, (d + 3) * rank : (d + 4) * rank]
+        ahead = [node // (NVX * NVX) >= NVX // 2, node // NVX % NVX >= NVX // 2]
+        sides = [jnp.where(ahead[d], plus[d], back[d]) for d in range(2)] + [plus[2], back[2]]
+        sliding = dot3(lnow, jnp.concatenate(sides, axis=1))
+        part = node_velocity(node + lax.broadcasted_iota(jnp.int32, (chunk, rank), 0))
+        slide = part[0] * sliding[:, :rank] + part[1] * sliding[:, rank : 2 * rank]
+        slide = slide + part[2] * jnp.where(part[2] > 0, sliding[:, 2 * rank : 3 * rank], sliding[:, 3 * rank :])
         mback = dot3(back_raw[span], turned)
-        lnew[span, :] = lnow + time_step * slide + COLLIDE * (mback - lnow)
-
-    new = lnew[...]
-    high, low = halves(new)
-    rest = (new - high.astype(F32) - low.astype(F32)).astype(BF16)
-    new_t = new.T
-    high_t, low_t = halves(new_t)
-    both = dot(high_t, jnp.concatenate([high, low, rest], axis=1))
-    mixed = both[:, rank : 2 * rank] + (both[:, 2 * rank :] + 0.5 * dot(low_t, low))
-    gram_v = (both[:, :rank] + (mixed + mixed.T)) * weight_v
+        new = lnow + time_step * slide + COLLIDE * (mback - lnow)
+        lnew[span, :] = new
+        high, low = halves(new)
+        rest = (new - high.astype(F32) - low.astype(F32)).astype(BF16)
+        high_t, low_t = halves(new.T)
+        both = dot(high_t, jnp.concatenate([high, low, rest], axis=1))
+        gram_v = gram_v + both[:, :rank]
+        mixed_v = mixed_v + (both[:, rank : 2 * rank] + (both[:, 2 * rank :] + 0.5 * dot(low_t, low)))
+    gram_v = (gram_v + (mixed_v + mixed_v.T)) * weight_v
+
     half_rank = rank // 2
     lanes = lax.broadcasted_iota(jnp.int32, (half_rank // 2, rank), 1)
     corner = jnp.where(
@@ -634,6 +684,9 @@
         for i, count in enumerate([members, members, layers, layers, members, members]):
             semaphores(name + "sem" + str(i), count - 1)
 
+    buffer("k_here", k_coeffs.shape)
+    buffer("v_here", v_basis.shape)
+    semaphores("insem", 2)
     buffer("vec", (slabs, 2 * layers, 8, rank))
     buffer("halo_a", (2, cells_y, cells_z, rank))
     buffer("halo_b", (2, cells_x, cells_z, rank))
@@ -686,13 +739,13 @@
             jax.ShapeDtypeStruct((rank, rank), F32),
             jax.ShapeDtypeStruct(v_basis.shape, F32),
         ),
-        in_specs=[VM, VM],
+        in_specs=[HBM, HBM],
         out_specs=(VM, VM, VM),
         scratch_shapes=scratch,
         compiler_params=pltpu.CompilerParams(
-            collective_id=1, has_side_effects=True, vmem_limit_bytes=min(60 * 2**20, used[0] + 10 * 2**20)
+            collective_id=1, has_side_effects=True, vmem_limit_bytes=min(62 * 2**20, used[0] + 14 * 2**20)
         ),
-    )(k_coeffs, v_basis)
+    )(pltpu.with_memory_space_constraint(k_coeffs, pltpu.HBM), pltpu.with_memory_space_constraint(v_basis, pltpu.HBM))
     chunks = 4
     basis_x, coupling, basis_v = pl.pallas_call(
         finish_kernel,
@@ -702,7 +755,7 @@
             jax.ShapeDtypeStruct(v_basis.shape, F32),
         ),
         in_specs=[VM, VM, VM],
-        out_specs=(ANY, ANY, ANY),
+        out_specs=(HBM, HBM, HBM),
         scratch_shapes=[
             pltpu.VMEM((rank, 2 * rank), F32),
             pltpu.VMEM((rank, rank), F32),

time: 86.9 us -> 76.8 us (0.88)
  Pallas kernels: 83.9 us -> 75.7 us
  local copies, waits for them, and re-layouts: 1.79 us -> 0 us
    pallas_call x1, Pallas kernels: 75.4 us -> 69.4 us  [local(): pl.pallas_call(functools.partial(step_kernel, tuple(names), slabs, layers...]
    pallas_call x1, Pallas kernels: 8.47 us -> 6.35 us  [local(): pl.pallas_call(finish_kernel, out_shape=(jax.ShapeDtypeStruct((own, rank)...]
    unnamed x4 -> x0, local copies, waits for them, and re-layouts: 1.79 us -> none
where the time goes in v3:
time: 76.8 us; the launch traced here: 76.5 us
  Pallas kernels  75.7 us (99%)
  between operations  0.8 us (1%)
    pallas_call x1, Pallas kernels, local(): pl.pallas_call(functools.partial(step_kernel, tuple(names), slabs, layers...  69.4 us
    pallas_call x1, Pallas kernels, local(): pl.pallas_call(finish_kernel, out_shape=(jax.ShapeDtypeStruct((own, rank)...  6.35 us

profile of v3, /device:TPU:0, one launch (start us, length us, event | category | flops | bytes accessed | tf_op | source)
XLA Modules:
  0.0 76.5 jit_solution(28353909844353997)
XLA Ops:
  0.6 69.4 %shard_map.49 = (f32[64,128]{1,0:T(8,128)S(1)}, f32[128,128]{1,0:T(8,128)S(1)}, f32[1024,128]{1,0:T(8,128)S(1)}) custom-call(f32[2,2,16,128]{3,2,1,0:T(8,128)} %refs_0_.1, f32[1024,128]{1,0:T(8,128)} %refs_1_.1), custom_call_target="tpu_custom_call" | custom-call | tf_op jit(solution)/shard_map/pallas_call | solution.py:735
  70.0 6.3 %shard_map.50 = (f32[64,128]{1,0:T(8,128)}, f32[128,128]{1,0:T(8,128)}, f32[1024,128]{1,0:T(8,128)}) custom-call(f32[128,128]{1,0:T(8,128)S(1)} %get-tuple-element.9.gram, f32[1024,128]{1,0:T(8,128)S(1)} %get-tuple-element.10.lnew, f32[64,128]{1,0:T(8,128)S(1)} %get-tuple-element.11.field), custom_call_target="tpu_custom_call" | custom-call | tf_op jit(solution)/shard_map/pallas_call | solution.py:750

commit v4 on v3

--- a/solution.py
+++ b/solution.py
@@ -68,52 +68,59 @@
 
 
 class Sum:
-    def __init__(self, send, pos, x, first, second, out, sems):
+    def __init__(self, send, pos, ref, name):
         self.send, self.pos = send, pos
-        self.x, self.first, self.second, self.out = x, first, second, out
-        self.sems = sems
-
-    def scatter(self):
-        me, members, member = self.pos.me, self.pos.members, self.pos.member
-        self.copies = []
-        for k in range(1, members):
-            to, device = member(k)
-            self.copies.append(
-                self.send(
-                    self.x.at[to], self.first.at[k - 1], self.sems[0].at[k - 1], self.sems[1].at[k - 1], device
-                )
-            )
-
-    def cross(self):
-        me, layer = self.pos.me, self.pos.layer
-        total = self.x[me]
-        for k, copy in enumerate(self.copies):
-            copy.wait_recv()
-            total = total + self.first[k]
-        self.second[layer] = total
-        mine = self.second.at[layer]
-        self.copies = [
-            self.send(mine, mine, self.sems[2].at[k - 1], self.sems[3].at[k - 1], self.pos.across(k))
-            for k in range(1, self.pos.layers)
+        self.x, self.first, self.half, self.second, self.third, self.out = [
+            ref[name + part] for part in ("x", "1", "h", "2", "3", "o")
         ]
-
-    def collect(self):
-        me = self.pos.me
+        self.sems = [(ref[name + part + "s"], ref[name + part + "r"]) for part in ("c", "s", "l", "g")]
+
+    def copy(self, source, target, stage, index, device):
+        sent, received = self.sems[stage]
+        return self.send(source, target, sent.at[index], received.at[index], device)
+
+    def wait(self):
         for copy in self.copies:
             copy.wait_recv()
+
+    def start(self):
+        self.copies = [self.copy(self.x.at[1 - self.pos.core], self.first, 0, 0, self.pos.partner())]
+
+    def scatter(self):
+        self.wait()
+        slab = self.pos.slab
+        self.half[...] = self.x[self.pos.core] + self.first[...]
+        self.second[slab] = self.half[slab]
+        self.copies = []
+        for k in range(1, self.pos.slabs):
+            to, device = self.pos.slab_at(k)
+            self.copies.append(self.copy(self.half.at[to], self.second.at[slab], 1, k - 1, device))
+
+    def cross(self):
+        self.wait()
         total = self.second[0]
+        for k in range(1, self.pos.slabs):
+            total = total + self.second[k]
+        self.third[self.pos.layer] = total
+        mine = self.third.at[self.pos.layer]
+        self.copies = [self.copy(mine, mine, 2, k - 1, self.pos.across(k)) for k in range(1, self.pos.layers)]
+
+    def collect(self):
+        self.wait()
+        total = self.third[0]
         for k in range(1, self.pos.layers):
-            total = total + self.second[k]
-        self.out[me] = total
-        mine = self.out.at[me]
-        self.copies = [
-            self.send(mine, mine, self.sems[4].at[k - 1], self.sems[5].at[k - 1], self.pos.member(k)[1])
-            for k in range(1, self.pos.members)
-        ]
+            total = total + self.third[k]
+        self.out[self.pos.core, self.pos.slab] = total
+        mine = self.out.at[self.pos.core, self.pos.slab]
+        self.copies = [self.copy(mine, mine, 3, k - 1, self.pos.slab_at(k)[1]) for k in range(1, self.pos.slabs)]
+
+    def share(self):
+        self.wait()
+        mine = self.out.at[self.pos.core]
+        self.copies = [self.copy(mine, mine, 0, 1, self.pos.partner())]
 
     def finish(self):
-        for copy in self.copies:
-            copy.wait_recv()
+        self.wait()
 
 
 class Position:
@@ -206,8 +213,13 @@
         both = jnp.concatenate(rows, axis=0)
         work[start : start + panel, :] = both
         if start + panel < size:
-            tall = both[:, :size].T[start + panel :, :]
-            work[start + panel :, :] = work[start + panel :, :] - dot6(tall, both)
+            high = both.astype(BF16).astype(F32)
+            low = (both - high).astype(BF16).astype(F32)
+            rest = both - high - low
+            left = jnp.concatenate([item[:, :size] for item in (high, high, low, high, rest, low)], axis=0)
+            right = jnp.concatenate([item.astype(BF16) for item in (high, low, high, rest, high, low)], axis=0)
+            tall = left.T[start + panel :, :].astype(BF16)
+            work[start + panel :, :] = work[start + panel :, :] - dot(tall, right)
     factor = jnp.where(column <= row, work[:, :size].T, 0.0)
     inverse = jnp.where(column <= row, work[:, size:], 0.0)
     return factor, inverse
@@ -250,7 +262,7 @@
         return copy
 
     barrier = pltpu.get_barrier_semaphore()
-    peers = [device for _, device in pos.others()]
+    peers = [pos.member(k)[1] for k in range(1, members)] + [pos.across(k) for k in range(1, layers)]
     for peer in peers:
         pl.semaphore_signal(barrier, inc=1, device_id=peer, device_id_type=MESH)
 
@@ -273,8 +285,8 @@
     squares = dot(upward.astype(BF16), jnp.concatenate(halves(values * values), axis=1))
     partial = sums[:, :rank] + (sums[:, rank : 2 * rank] + sums[:, 2 * rank :])
     partial = (partial + (squares[:, :rank] + squares[:, rank:])) * weight_v
-    vec = ref["vec"]
-    vec[slab, brick] = partial
+    vec_l, vec_m = ref["vec_l"], ref["vec_m"]
+    vec_l[layer] = partial
 
     turned_v = values.T
     vt_high, vt_low = halves(turned_v)
@@ -296,28 +308,32 @@
 
     pack(0)
     pl.semaphore_wait(barrier, len(peers))
-    mine = vec.at[slab, brick]
-    copies = [send(mine, mine, ref["vs"].at[i], ref["vr"].at[i], device) for i, device in pos.others()]
-    halo_a, halo_b = ref["halo_a"], ref["halo_b"]
-    halos = [
-        send(k_ref.at[cells_x - 1], halo_a.at[0], ref["hs"].at[0], ref["hr"].at[0], pos.slab_at(1)[1]),
-        send(k_ref.at[0], halo_a.at[1], ref["hs"].at[1], ref["hr"].at[1], pos.slab_at(slabs - 1)[1]),
-        send(k_ref.at[:, cells_y - 1], halo_b.at[0], ref["hs"].at[2], ref["hr"].at[2], pos.brick_at(1)),
-        send(k_ref.at[:, 0], halo_b.at[1], ref["hs"].at[3], ref["hr"].at[3], pos.brick_at(-1)),
+    mine = vec_l.at[layer]
+    copies = [
+        send(mine, mine, ref["vls"].at[k - 1], ref["vlr"].at[k - 1], pos.across(k)) for k in range(1, layers)
     ]
-
     pack(1)
     pack(2)
-    share = 3 * rank // members
-    ref["tx"][...] = jnp.concatenate(packed, axis=0).reshape(members, share, rank)
-    transport_sum = Sum(send, pos, ref["tx"], ref["t1"], ref["t2"], ref["to"], [ref[f"tsem{i}"] for i in range(6)])
+    ref["tx"][...] = jnp.concatenate(packed, axis=0).reshape(ref["tx"].shape)
+    transport_sum = Sum(send, pos, ref, "t")
+
+    for copy in copies:
+        copy.wait_recv()
+    total = vec_l[0]
+    for k in range(1, layers):
+        total = total + vec_l[k]
+    vec_m[me] = total
+    mine = vec_m.at[me]
+    copies = [
+        send(mine, mine, ref["vms"].at[k - 1], ref["vmr"].at[k - 1], pos.member(k)[1]) for k in range(1, members)
+    ]
+    transport_sum.start()
     transport_sum.scatter()
-
     for copy in copies:
         copy.wait_recv()
-    vectors = vec[0, 0]
-    for k in range(1, slabs * bricks):
-        vectors = vectors + vec[k // bricks, k % bricks]
+    vectors = vec_m[0]
+    for k in range(1, members):
+        vectors = vectors + vec_m[k]
 
     own_k = k_ref[...].reshape(own, rank)
     kpad = ref["kpad"]
@@ -341,11 +357,18 @@
     inside = (lane_pair >= core * own) & (lane_pair < (core + 1) * own)
     par = ref["par"]
     par[me, layer] = jnp.where(inside, state, 0.0)
-    mine = par.at[me, layer]
+    mine = par.at[me, layer, pl.ds(0, 5)]
     copies = [send(mine, mine, ref["ps"].at[i], ref["pr"].at[i], device) for i, device in pos.others()]
+    halo_a, halo_b = ref["halo_a"], ref["halo_b"]
+    halos = [
+        send(k_ref.at[cells_x - 1], halo_a.at[0], ref["hs"].at[0], ref["hr"].at[0], pos.slab_at(1)[1]),
+        send(k_ref.at[0], halo_a.at[1], ref["hs"].at[1], ref["hr"].at[1], pos.slab_at(slabs - 1)[1]),
+        send(k_ref.at[:, cells_y - 1], halo_b.at[0], ref["hs"].at[2], ref["hr"].at[2], pos.brick_at(1)),
+        send(k_ref.at[:, 0], halo_b.at[1], ref["hs"].at[3], ref["hr"].at[3], pos.brick_at(-1)),
+    ]
+    transport_sum.cross()
     for copy in copies:
         copy.wait_recv()
-    transport_sum.cross()
 
     mt_high, mt_low = ref["mt_high"], ref["mt_low"]
     mp, first, half, second, third = ref["mp"], ref["first"], ref["half"], ref["second"], ref["third"]
@@ -400,12 +423,14 @@
         to = lax.rem(slab + k, slabs)
         for slot in range(slots):
             project(to, slot)
+            if k == 1 and slot == 0:
+                transport_sum.collect()
             copy = hand_over(k, slot, to)
             if len(waiting) >= 1:
                 hand_on(*waiting.pop(0))
             waiting.append((k, slot, to, copy))
 
-    transport_sum.collect()
+    transport_sum.share()
     for copy in waiting:
         hand_on(*copy)
 
@@ -494,8 +519,9 @@
     ]
     crossing = [to_slabs(here, 0)]
     last = [send(here, here, ref["ds"].at[0, 0], ref["dr"].at[0, 0], pos.partner())]
-    raw_sum = Sum(send, pos, ref["rx"], ref["r1"], ref["r2"], ref["ro"], [ref[f"rsem{i}"] for i in range(6)])
-    ref["rx"][...] = dot3(advanced.T, mproj).reshape(members, rank // members, rank)
+    raw_sum = Sum(send, pos, ref, "r")
+    ref["rx"][...] = dot3(advanced.T, mproj).reshape(ref["rx"].shape)
+    raw_sum.start()
     raw_sum.scatter()
     for j in range(1, layers):
         along[j - 1].wait_recv()
@@ -542,6 +568,7 @@
     both = dot(at[...], d_high[...])
     slopes = both[:rank] + (both[rank:] + dot(at[:rank], d_low[...]))
     slopes = [slopes[:, d * rank : (d + 1) * rank] * (lengths[d] * weight_x) for d in range(3)]
+    raw_sum.share()
     raw_sum.finish()
     raw = ref["ro"][...].reshape(rank, rank) * weight_x
     source = time_step * dot6(
@@ -677,17 +704,21 @@
         scratch.append(pltpu.SemaphoreType.DMA(shape))
 
     def reduction(name, rows):
-        buffer(name + "x", (members, rows, rank))
-        buffer(name + "1", (members - 1, rows, rank))
-        buffer(name + "2", (layers, rows, rank))
-        buffer(name + "o", (members, rows, rank))
-        for i, count in enumerate([members, members, layers, layers, members, members]):
-            semaphores(name + "sem" + str(i), count - 1)
+        buffer(name + "x", (2, slabs, rows, rank))
+        buffer(name + "1", (slabs, rows, rank))
+        buffer(name + "h", (slabs, rows, rank))
+        buffer(name + "2", (slabs, rows, rank))
+        buffer(name + "3", (layers, rows, rank))
+        buffer(name + "o", (2, slabs, rows, rank))
+        for stage, count in (("c", 2), ("s", slabs - 1), ("l", layers - 1), ("g", slabs - 1)):
+            semaphores(name + stage + "s", count)
+            semaphores(name + stage + "r", count)
 
     buffer("k_here", k_coeffs.shape)
     buffer("v_here", v_basis.shape)
     semaphores("insem", 2)
-    buffer("vec", (slabs, 2 * layers, 8, rank))
+    buffer("vec_l", (layers, 8, rank))
+    buffer("vec_m", (members, 8, rank))
     buffer("halo_a", (2, cells_y, cells_z, rank))
     buffer("halo_b", (2, cells_x, cells_z, rank))
     buffer("vt", (2 * rank, nodes), BF16)
@@ -716,7 +747,7 @@
     buffer("g2", (slabs, packed, rank))
     buffer("g3", (layers, packed, rank))
     buffer("go", (2, packed, rank))
-    for name, count in (("gc", 2), ("gs", slabs - 1), ("v", devices - 1), ("p", devices - 1)):
+    for name, count in (("gc", 2), ("gs", slabs - 1), ("vl", layers - 1), ("vm", members - 1), ("p", devices - 1)):
         semaphores(name + "s", count)
         semaphores(name + "r", count)
     for name in ("gl", "z", "a"):

time: 76.8 us -> 73.9 us (0.962)
  Pallas kernels: 75.7 us -> 72.8 us
    pallas_call x1, Pallas kernels: 69.4 us -> 67 us  [local(): pl.pallas_call(functools.partial(step_kernel, tuple(names), slabs, layers...]
where the time goes in v4:
time: 73.9 us; the launch traced here: 73.6 us
  Pallas kernels  72.8 us (99%)
  between operations  0.8 us (1%)
    pallas_call x1, Pallas kernels, local(): pl.pallas_call(functools.partial(step_kernel, tuple(names), slabs, layers...  67 us
    pallas_call x1, Pallas kernels, local(): pl.pallas_call(finish_kernel, out_shape=(jax.ShapeDtypeStruct((own, rank)...  5.76 us

profile of v4, /device:TPU:0, one launch (start us, length us, event | category | flops | bytes accessed | tf_op | source)
XLA Modules:
  0.0 73.6 jit_solution(4250968649866070184)
XLA Ops:
  0.6 67.0 %shard_map.49 = (f32[64,128]{1,0:T(8,128)S(1)}, f32[128,128]{1,0:T(8,128)S(1)}, f32[1024,128]{1,0:T(8,128)S(1)}) custom-call(f32[2,2,16,128]{3,2,1,0:T(8,128)} %refs_0_.1, f32[1024,128]{1,0:T(8,128)} %refs_1_.1), custom_call_target="tpu_custom_call" | custom-call | tf_op jit(solution)/shard_map/pallas_call | solution.py:766
  67.7 5.8 %shard_map.50 = (f32[64,128]{1,0:T(8,128)}, f32[128,128]{1,0:T(8,128)}, f32[1024,128]{1,0:T(8,128)}) custom-call(f32[128,128]{1,0:T(8,128)S(1)} %get-tuple-element.9.gram, f32[1024,128]{1,0:T(8,128)S(1)} %get-tuple-element.10.lnew, f32[64,128]{1,0:T(8,128)S(1)} %get-tuple-element.11.field), custom_call_target="tpu_custom_call" | custom-call | tf_op jit(solution)/shard_map/pallas_call | solution.py:781

commit v5 on v4

--- a/solution.py
+++ b/solution.py
@@ -52,8 +52,22 @@
     return both[:, :width] + both[:, width:]
 
 
+def thirds(values):
+    high = values.astype(BF16)
+    rest = values - high.astype(F32)
+    middle = rest.astype(BF16)
+    return high, middle, (rest - middle.astype(F32)).astype(BF16)
+
+
 def dot6(left, right):
-    return jnp.dot(left, right, precision=PRECISE, preferred_element_type=F32)
+    width = right.shape[1]
+    high, middle, low = thirds(left)
+    right_high, right_middle, right_low = thirds(right)
+    top = jnp.concatenate([right_high, right_low], axis=1)
+    under = jnp.concatenate([right_high, right_middle], axis=1)
+    both = dot(jnp.concatenate([high, middle], axis=1), jnp.concatenate([top, under], axis=0))
+    cross = dot(jnp.concatenate([high, low], axis=1), jnp.concatenate([right_middle, right_high], axis=0))
+    return both[:, :width] + (cross + both[:, width:])
 
 
 def node_velocity(indices):
@@ -166,12 +180,22 @@
         to = lax.rem(self.slab + k, self.slabs)
         return to, (to, self.brick)
 
+    def slab_mate(self, k):
+        if self.slabs != 4 or k == 0:
+            return lax.rem(self.slab + k, self.slabs)
+        if k == 1:
+            return self.slabs - 1 - self.slab
+        return self.slab + 1 - 2 * lax.rem(self.slab, 2) if k == 2 else lax.rem(self.slab + 2, self.slabs)
+
+    def slab_source(self, k):
+        return self.slab_mate(k) if self.slabs == 4 else lax.rem(self.slab + self.slabs - k, self.slabs)
+
     def brick_at(self, k):
         bricks = 2 * self.layers
         return (self.slab, lax.rem(self.brick + k + bricks, bricks))
 
 
-def factor_steps(work, matrix):
+def factor_steps(work, matrix, fillers=()):
     size = matrix.shape[0]
     block, panel = 8, 16
     row = lax.broadcasted_iota(jnp.int32, (size, size), 0)
@@ -180,7 +204,10 @@
     work[:, size:] = jnp.where(row == column, 1.0, 0.0)
     sub = lax.broadcasted_iota(jnp.int32, (block, size), 0)
     narrow, wide = (block, size), (block, 2 * size)
+    fillers = list(fillers)
     for start in range(0, size, panel):
+        if fillers:
+            fillers.pop(0)()
         rows = [work[start : start + block, :], work[start + block : start + panel, :]]
         for b in range(2):
             at = start + b * block
@@ -220,6 +247,8 @@
             right = jnp.concatenate([item.astype(BF16) for item in (high, low, high, rest, high, low)], axis=0)
             tall = left.T[start + panel :, :].astype(BF16)
             work[start + panel :, :] = work[start + panel :, :] - dot(tall, right)
+    for filler in fillers:
+        filler()
     factor = jnp.where(column <= row, work[:, :size].T, 0.0)
     inverse = jnp.where(column <= row, work[:, size:], 0.0)
     return factor, inverse
@@ -306,17 +335,17 @@
             sides.append(both[:, :rank] + (both[:, rank:] + dot(low, v_high)))
         packed.append(jnp.where(row > column, sides[0], sides[1]))
 
-    pack(0)
+    for d in range(3):
+        pack(d)
+    ref["tx"][...] = jnp.concatenate(packed, axis=0).reshape(ref["tx"].shape)
+    transport_sum = Sum(send, pos, ref, "t")
     pl.semaphore_wait(barrier, len(peers))
     mine = vec_l.at[layer]
     copies = [
         send(mine, mine, ref["vls"].at[k - 1], ref["vlr"].at[k - 1], pos.across(k)) for k in range(1, layers)
     ]
-    pack(1)
-    pack(2)
-    ref["tx"][...] = jnp.concatenate(packed, axis=0).reshape(ref["tx"].shape)
-    transport_sum = Sum(send, pos, ref, "t")
-
+    transport_sum.start()
+    transport_sum.scatter()
     for copy in copies:
         copy.wait_recv()
     total = vec_l[0]
@@ -327,8 +356,7 @@
     copies = [
         send(mine, mine, ref["vms"].at[k - 1], ref["vmr"].at[k - 1], pos.member(k)[1]) for k in range(1, members)
     ]
-    transport_sum.start()
-    transport_sum.scatter()
+    transport_sum.cross()
     for copy in copies:
         copy.wait_recv()
     vectors = vec_m[0]
@@ -366,7 +394,7 @@
         send(k_ref.at[:, cells_y - 1], halo_b.at[0], ref["hs"].at[2], ref["hr"].at[2], pos.brick_at(1)),
         send(k_ref.at[:, 0], halo_b.at[1], ref["hs"].at[3], ref["hr"].at[3], pos.brick_at(-1)),
     ]
-    transport_sum.cross()
+    transport_sum.collect()
     for copy in copies:
         copy.wait_recv()
 
@@ -386,13 +414,14 @@
         rate, scale = state[3:4], state[4:5]
         fast = jnp.exp((fast_v[2] - u[2]) ** 2 * rate)
         slow = jnp.exp(((slow_v[0] - u[0]) ** 2 + (slow_v[1] - u[1]) ** 2) * rate) * scale
-        place = pl.ds(pl.multiple_of((to * slots + slot) * width, width), width)
+        places = [pl.ds(pl.multiple_of(((2 * slot + i) * slabs + to) * pair, pair), pair) for i in range(2)]
         for t in range(groups):
             high, low = halves(fast * slow[t : t + 1])
-            mt_high[t * group : (t + 1) * group, place] = high
-            mt_low[t * group : (t + 1) * group, place] = low
-        high = dot(vt[...], mt_high[:, place])
-        low = dot(vt[:rank], mt_low[:, place])
+            for i, place in enumerate(places):
+                mt_high[t * group : (t + 1) * group, place] = high[:, i * pair : (i + 1) * pair]
+                mt_low[t * group : (t + 1) * group, place] = low[:, i * pair : (i + 1) * pair]
+        high = dot(vt[...], jnp.concatenate([mt_high[:, place] for place in places], axis=1))
+        low = dot(vt[:rank], jnp.concatenate([mt_low[:, place] for place in places], axis=1))
         result = ((high[:rank] + (high[rank:] + low)) * weight_v).T
         for i in range(2):
             for c in range(2):
@@ -420,17 +449,16 @@
 
     waiting = []
     for k in list(range(1, slabs)) + [0]:
-        to = lax.rem(slab + k, slabs)
+        to = pos.slab_mate(k)
         for slot in range(slots):
             project(to, slot)
             if k == 1 and slot == 0:
-                transport_sum.collect()
+                transport_sum.share()
             copy = hand_over(k, slot, to)
             if len(waiting) >= 1:
                 hand_on(*waiting.pop(0))
             waiting.append((k, slot, to, copy))
 
-    transport_sum.share()
     for copy in waiting:
         hand_on(*copy)
 
@@ -504,12 +532,12 @@
     advanced = kept + COLLIDE * mproj
 
     adv = ref["adv"]
-    adv[slab, brick] = advanced.reshape(cells_x, cells_y, cells_z, rank)
-    here = adv.at[slab, brick]
+    adv[layer, slab, core] = advanced.reshape(cells_x, cells_y, cells_z, rank)
+    here = adv.at[layer, slab, core]
 
     def to_slabs(block, j):
         return [
-            send(block, block, ref["bs"].at[k - 1, j], ref["br"].at[k - 1, j], pos.slab_at(k)[1])
+            send(block, block, ref["bs"].at[k - 1, j], ref["br"].at[k - 1, j], (pos.slab_mate(k), brick))
             for k in range(1, slabs)
         ]
 
@@ -518,68 +546,105 @@
         for k in range(1, layers)
     ]
     crossing = [to_slabs(here, 0)]
-    last = [send(here, here, ref["ds"].at[0, 0], ref["dr"].at[0, 0], pos.partner())]
+    last = [[send(here, here, ref["ds"].at[0, 0], ref["dr"].at[0, 0], pos.partner())]]
     raw_sum = Sum(send, pos, ref, "r")
     ref["rx"][...] = dot3(advanced.T, mproj).reshape(ref["rx"].shape)
     raw_sum.start()
     raw_sum.scatter()
     for j in range(1, layers):
         along[j - 1].wait_recv()
-        block = adv.at[slab, 2 * pos.source(j) + core]
+        block = adv.at[pos.source(j), slab, core]
         crossing.append(to_slabs(block, j))
-        last.append(send(block, block, ref["ds"].at[0, j], ref["dr"].at[0, j], pos.partner()))
-    raw_sum.cross()
-    for j in range(layers):
+        last.append([send(block, block, ref["ds"].at[0, j], ref["dr"].at[0, j], pos.partner())])
+
+    at, ahl, back = ref["at"], ref["ahl"], ref["back"]
+    d_high, d_low, gram_l = ref["d_high"], ref["d_low"], ref["gram_l"]
+    plane = cells // layers
+
+    def relay(j):
         for k in range(1, slabs):
             crossing[j][k - 1].wait_recv()
-            block = adv.at[lax.rem(slab + slabs - k, slabs), 2 * pos.source(j) + core]
-            last.append(send(block, block, ref["ds"].at[k, j], ref["dr"].at[k, j], pos.partner()))
-    raw_sum.collect()
-    for copy in last:
-        copy.wait_recv()
-
-    at, ahl = ref["at"], ref["ahl"]
-    d_high, d_low = ref["d_high"], ref["d_low"]
-    plane = cells // slabs
-    for s in range(slabs):
-        block = adv[s]
+            block = adv.at[pos.source(j), pos.slab_source(k), core]
+            last[j].append(send(block, block, ref["ds"].at[k, j], ref["dr"].at[k, j], pos.partner()))
+
+    def store_slopes(span, d, values):
+        high, low = halves(values)
+        d_high[span, d * rank : (d + 1) * rank] = high
+        d_low[span, d * rank : (d + 1) * rank] = low
+
+    def take(j):
+        for copy in last[j]:
+            copy.wait_recv()
+        from_layer = pos.source(j)
+        block = adv[from_layer]
+        span = pl.ds(pl.multiple_of(from_layer * plane, plane), plane)
         flat = block.reshape(plane, rank)
-        span = slice(s * plane, (s + 1) * plane)
         high, low = halves(flat)
         ahl[span, :rank] = high
         ahl[span, rank:] = low
-        high, low = halves(flat.T)
-        at[:rank, span] = high
-        at[rank:, span] = low
-        following = adv[(s + 1) % slabs]
-        up_a = jnp.concatenate([block[:, 1:], following[:, :1]], axis=1)
-        wrapped = jnp.concatenate([block[1:, :, :1], block[:1, :, :1]], axis=0)
-        up_b = jnp.concatenate([block[:, :, 1:], wrapped], axis=2)
-        ups = [up_a.reshape(plane, rank), up_b.reshape(plane, rank), next_third(flat)]
-        for d in range(3):
-            high, low = halves(ups[d] - flat)
-            d_high[span, d * rank : (d + 1) * rank] = high
-            d_low[span, d * rank : (d + 1) * rank] = low
-    both = dot(at[:rank], ahl[...])
-    mixed = both[:, rank:]
-    gram = (both[:, :rank] + (mixed + mixed.T)) * weight_x
-    factor, inverse = factor_steps(ref["work"], gram)
-
-    both = dot(at[...], d_high[...])
-    slopes = both[:rank] + (both[rank:] + dot(at[:rank], d_low[...]))
-    slopes = [slopes[:, d * rank : (d + 1) * rank] * (lengths[d] * weight_x) for d in range(3)]
-    raw_sum.share()
-    raw_sum.finish()
-    raw = ref["ro"][...].reshape(rank, rank) * weight_x
-    source = time_step * dot6(
-        jnp.concatenate(slopes + [-item.T for item in slopes], axis=1), trans[...]
-    ) - COLLIDE * raw
-
-    place = 2 * own
-    scaled = ahl[...]
-    top = dot(mt_high[...], scaled)
-    low = dot(mt_low[...], ahl[:, :rank])
-    back_raw = (top[:, :rank] + (top[:, rank:] + low)) * weight_x
+        high_t, low_t = halves(flat.T)
+        at[:rank, span] = high_t
+        at[rank:, span] = low_t
+        gram_l[from_layer] = dot(high_t, jnp.concatenate([high, low], axis=1))
+        across = jnp.concatenate([block[1:, :, :1], block[:1, :, :1]], axis=0)
+        after = jnp.concatenate([block[:, :, 1:], across], axis=2)
+        store_slopes(span, 0, after.reshape(plane, rank) - flat)
+        store_slopes(span, 2, next_third(flat) - flat)
+
+    def project_back(j, rows):
+        span = pl.ds(pl.multiple_of(pos.source(j) * plane, plane), plane)
+        top = dot(mt_high[rows, span], ahl[span, :])
+        part = top[:, :rank] + (top[:, rank:] + dot(mt_low[rows, span], ahl[span, :rank]))
+        back[rows, :] = part if j == 0 else back[rows, :] + part
+
+    quarters = [slice(i * (nodes // 4), (i + 1) * (nodes // 4)) for i in range(4)]
+    for j in range(layers):
+        relay(j)
+        if j == 1:
+            raw_sum.cross()
+        if j > 0:
+            take(j - 1)
+            for rows in quarters:
+                project_back(j - 1, rows)
+    raw_sum.collect()
+    take(layers - 1)
+    total = gram_l[0]
+    for k in range(1, layers):
+        total = total + gram_l[k]
+    mixed = total[:, rank:]
+    gram = (total[:, :rank] + (mixed + mixed.T)) * weight_x
+    for k in range(layers):
+        block, following = adv[k], adv[(k + 1) % layers]
+        ups = [
+            jnp.concatenate([block[:, 0, :, 1:], block[:, 1, :, :1]], axis=2),
+            jnp.concatenate([block[:, 1, :, 1:], following[:, 0, :, :1]], axis=2),
+        ]
+        for c in range(2):
+            difference = (ups[c] - block[:, c]).reshape(slabs, own, rank)
+            for i in range(slabs):
+                first_row = k * plane + (2 * i + c) * own
+                store_slopes(slice(first_row, first_row + own), 1, difference[i])
+    slopes = [None] * 3
+
+    def slope_product(d):
+        columns = slice(d * rank, (d + 1) * rank)
+        both = dot(at[...], d_high[:, columns])
+        both = both[:rank] + (both[rank:] + dot(at[:rank], d_low[:, columns]))
+        slopes[d] = both * (lengths[d] * weight_x)
+
+    sources = []
+
+    def drive():
+        sources.append(
+            time_step * dot6(jnp.concatenate(slopes + [-item.T for item in slopes], axis=1), trans[...])
+        )
+
+    back_last = [functools.partial(project_back, layers - 1, rows) for rows in quarters]
+    fillers = [functools.partial(slope_product, d) for d in (0, 2, 1)] + [drive]
+    fillers += [back_last[0], lambda: (raw_sum.share(), back_last[1]()), back_last[2]]
+    fillers += [lambda: (raw_sum.finish(), back_last[3]())]
+    factor, inverse = factor_steps(ref["work"], gram, fillers)
+    source = sources[0] - COLLIDE * weight_x * ref["ro"][...].reshape(rank, rank)
 
     turned = inverse.T
     middle = (1.0 + COLLIDE) * factor + dot6(source.T, turned)
@@ -590,18 +655,18 @@
     chunk = math.gcd(nodes, NVX * NVX // 4)
     gram_v = jnp.zeros((rank, rank), F32)
     mixed_v = jnp.zeros((rank, rank), F32)
-    back = [-item.T for item in plus]
+    behind = [-item.T for item in plus]
     for at_row in range(0, nodes, chunk):
         span = slice(at_row, at_row + chunk)
         node = base + at_row
         lnow = dot3(v_ref[span, :], middle)
         ahead = [node // (NVX * NVX) >= NVX // 2, node // NVX % NVX >= NVX // 2]
-        sides = [jnp.where(ahead[d], plus[d], back[d]) for d in range(2)] + [plus[2], back[2]]
+        sides = [jnp.where(ahead[d], plus[d], behind[d]) for d in range(2)] + [plus[2], behind[2]]
         sliding = dot3(lnow, jnp.concatenate(sides, axis=1))
         part = node_velocity(node + lax.broadcasted_iota(jnp.int32, (chunk, rank), 0))
         slide = part[0] * sliding[:, :rank] + part[1] * sliding[:, rank : 2 * rank]
         slide = slide + part[2] * jnp.where(part[2] > 0, sliding[:, 2 * rank : 3 * rank], sliding[:, 3 * rank :])
-        mback = dot3(back_raw[span], turned)
+        mback = dot3(back[span, :] * weight_x, turned)
         new = lnow + time_step * slide + COLLIDE * (mback - lnow)
         lnew[span, :] = new
         high, low = halves(new)
@@ -733,7 +798,9 @@
     buffer("quarter", (layers, own, rank))
     buffer("third", (layers, own, rank))
     buffer("trans", (6 * rank, rank))
-    buffer("adv", (slabs, 2 * layers, cells_x, cells_y, cells_z, rank))
+    buffer("adv", (layers, slabs, 2, cells_x, cells_y, cells_z, rank))
+    buffer("back", (nodes, rank))
+    buffer("gram_l", (layers, rank, 2 * rank))
     buffer("at", (2 * rank, cells), BF16)
     buffer("ahl", (cells, 2 * rank), BF16)
     buffer("d_high", (cells, 3 * rank), BF16)

time: 73.9 us -> 70.7 us (0.957)
  Pallas kernels: 72.8 us -> 69.7 us
    pallas_call x1, Pallas kernels: 67 us -> 63.9 us  [local(): pl.pallas_call(functools.partial(step_kernel, tuple(names), slabs, layers...]
where the time goes in v5:
time: 70.7 us; the launch traced here: 70.5 us
  Pallas kernels  69.7 us (99%)
  between operations  0.8 us (1%)
    pallas_call x1, Pallas kernels, local(): pl.pallas_call(functools.partial(step_kernel, tuple(names), slabs, layers...  63.9 us
    pallas_call x1, Pallas kernels, local(): pl.pallas_call(finish_kernel, out_shape=(jax.ShapeDtypeStruct((own, rank)...  5.76 us

profile of v5, /device:TPU:0, one launch (start us, length us, event | category | flops | bytes accessed | tf_op | source)
XLA Modules:
  0.0 70.5 jit_solution(12549077805324889630)
XLA Ops:
  0.6 63.9 %shard_map.49 = (f32[64,128]{1,0:T(8,128)S(1)}, f32[128,128]{1,0:T(8,128)S(1)}, f32[1024,128]{1,0:T(8,128)S(1)}) custom-call(f32[2,2,16,128]{3,2,1,0:T(8,128)} %refs_0_.1, f32[1024,128]{1,0:T(8,128)} %refs_1_.1), custom_call_target="tpu_custom_call" | custom-call | tf_op jit(solution)/shard_map/pallas_call | solution.py:833
  64.6 5.8 %shard_map.50 = (f32[64,128]{1,0:T(8,128)}, f32[128,128]{1,0:T(8,128)}, f32[1024,128]{1,0:T(8,128)}) custom-call(f32[128,128]{1,0:T(8,128)S(1)} %get-tuple-element.9.gram, f32[1024,128]{1,0:T(8,128)S(1)} %get-tuple-element.10.lnew, f32[64,128]{1,0:T(8,128)S(1)} %get-tuple-element.11.field), custom_call_target="tpu_custom_call" | custom-call | tf_op jit(solution)/shard_map/pallas_call | solution.py:848

commit v6 on v5

--- a/solution.py
+++ b/solution.py
@@ -407,7 +407,7 @@
     fast_v = node_velocity(base + lax.broadcasted_iota(jnp.int32, (group, width), 0))
     slow_v = node_velocity(base + group * lax.broadcasted_iota(jnp.int32, (groups, width), 0))
 
-    def project(to, slot):
+    def build(to, slot, stage):
         blocks = [par[2 * to, 2 * slot + i] + par[2 * to + 1, 2 * slot + i] for i in range(2)]
         state = jnp.concatenate(blocks, axis=1)
         u = [state[d : d + 1] for d in range(3)]
@@ -417,11 +417,16 @@
         places = [pl.ds(pl.multiple_of(((2 * slot + i) * slabs + to) * pair, pair), pair) for i in range(2)]
         for t in range(groups):
             high, low = halves(fast * slow[t : t + 1])
+            span = slice(t * group, (t + 1) * group)
+            stage[0][span, :] = high
+            stage[1][span, :] = low
             for i, place in enumerate(places):
-                mt_high[t * group : (t + 1) * group, place] = high[:, i * pair : (i + 1) * pair]
-                mt_low[t * group : (t + 1) * group, place] = low[:, i * pair : (i + 1) * pair]
-        high = dot(vt[...], jnp.concatenate([mt_high[:, place] for place in places], axis=1))
-        low = dot(vt[:rank], jnp.concatenate([mt_low[:, place] for place in places], axis=1))
+                mt_high[span, place] = high[:, i * pair : (i + 1) * pair]
+                mt_low[span, place] = low[:, i * pair : (i + 1) * pair]
+
+    def multiply(to, slot, stage):
+        high = dot(vt[...], stage[0][...])
+        low = dot(vt[:rank], stage[1][...])
         result = ((high[:rank] + (high[rank:] + low)) * weight_v).T
         for i in range(2):
             for c in range(2):
@@ -448,16 +453,19 @@
         )
 
     waiting = []
-    for k in list(range(1, slabs)) + [0]:
-        to = pos.slab_mate(k)
-        for slot in range(slots):
-            project(to, slot)
-            if k == 1 and slot == 0:
-                transport_sum.share()
-            copy = hand_over(k, slot, to)
-            if len(waiting) >= 1:
-                hand_on(*waiting.pop(0))
-            waiting.append((k, slot, to, copy))
+    steps = [(k, pos.slab_mate(k), slot) for k in list(range(1, slabs)) + [0] for slot in range(slots)]
+    stages = [(ref["stage_h0"], ref["stage_l0"]), (ref["stage_h1"], ref["stage_l1"])]
+    build(*steps[0][1:], stages[0])
+    for i, (k, to, slot) in enumerate(steps):
+        multiply(to, slot, stages[i % 2])
+        if i + 1 < len(steps):
+            build(*steps[i + 1][1:], stages[(i + 1) % 2])
+        copy = hand_over(k, slot, to)
+        if i == 0:
+            transport_sum.share()
+        if len(waiting) >= 2:
+            hand_on(*waiting.pop(0))
+        waiting.append((k, slot, to, copy))
 
     for copy in waiting:
         hand_on(*copy)
@@ -694,6 +702,9 @@
         send(mine, mine, ref["gss"].at[k - 1], ref["gsr"].at[k - 1], pos.slab_at(k)[1]) for k in range(1, slabs)
     ]
     ref["basis_x"][...] = dot3(advanced, turned)
+    sent = len(started) - len(copies)
+    for copy in started[:sent]:
+        copy.wait_send()
     for copy in copies:
         copy.wait_recv()
     total = g2[0]
@@ -718,7 +729,7 @@
     gram_ref[:half_rank] = whole[:half_rank]
     gram_ref[half_rank : half_rank + half_rank // 2] = pltpu.roll(corner, half_rank, 1)
     gram_ref[half_rank + half_rank // 2 :] = corner
-    for copy in started:
+    for copy in started[sent:]:
         copy.wait_send()
 
 
@@ -791,6 +802,8 @@
     buffer("par", (members, layers, 8, pair))
     buffer("mt_high", (nodes, cells), BF16)
     buffer("mt_low", (nodes, cells), BF16)
+    for name in ("stage_h0", "stage_l0", "stage_h1", "stage_l1"):
+        buffer(name, (nodes, 2 * pair), BF16)
     buffer("mp", (slabs, layers, 2, own, rank))
     buffer("first", (slabs, layers, own, rank))
     buffer("half", (slabs, layers, own, rank))

time: 70.7 us -> 70.5 us (level)
  no operation moved by 1% of the time
where the time goes in v6:
time: 70.5 us; the launch traced here: 70.3 us
  Pallas kernels  69.5 us (99%)
  between operations  0.8 us (1%)
    pallas_call x1, Pallas kernels, local(): pl.pallas_call(functools.partial(step_kernel, tuple(names), slabs, layers...  63.8 us
    pallas_call x1, Pallas kernels, local(): pl.pallas_call(finish_kernel, out_shape=(jax.ShapeDtypeStruct((own, rank)...  5.76 us

profile of v6, /device:TPU:0, one launch (start us, length us, event | category | flops | bytes accessed | tf_op | source)
XLA Modules:
  0.0 70.3 jit_solution(11195027769244325857)
XLA Ops:
  0.6 63.8 %shard_map.49 = (f32[64,128]{1,0:T(8,128)S(1)}, f32[128,128]{1,0:T(8,128)S(1)}, f32[1024,128]{1,0:T(8,128)S(1)}) custom-call(f32[2,2,16,128]{3,2,1,0:T(8,128)} %refs_0_.1, f32[1024,128]{1,0:T(8,128)} %refs_1_.1), custom_call_target="tpu_custom_call" | custom-call | tf_op jit(solution)/shard_map/pallas_call | solution.py:846
  64.4 5.8 %shard_map.50 = (f32[64,128]{1,0:T(8,128)}, f32[128,128]{1,0:T(8,128)}, f32[1024,128]{1,0:T(8,128)}) custom-call(f32[128,128]{1,0:T(8,128)S(1)} %get-tuple-element.9.gram, f32[1024,128]{1,0:T(8,128)S(1)} %get-tuple-element.10.lnew, f32[64,128]{1,0:T(8,128)S(1)} %get-tuple-element.11.field), custom_call_target="tpu_custom_call" | custom-call | tf_op jit(solution)/shard_map/pallas_call | solution.py:861

commit v7 on v6

--- a/solution.py
+++ b/solution.py
@@ -185,7 +185,7 @@
             return lax.rem(self.slab + k, self.slabs)
         if k == 1:
             return self.slabs - 1 - self.slab
-        return self.slab + 1 - 2 * lax.rem(self.slab, 2) if k == 2 else lax.rem(self.slab + 2, self.slabs)
+        return self.slab + 1 - 2 * lax.rem(self.slab, 2) if k == 3 else lax.rem(self.slab + 2, self.slabs)
 
     def slab_source(self, k):
         return self.slab_mate(k) if self.slabs == 4 else lax.rem(self.slab + self.slabs - k, self.slabs)
@@ -612,7 +612,7 @@
             raw_sum.cross()
         if j > 0:
             take(j - 1)
-            for rows in quarters:
+            for rows in quarters if j < layers - 1 else ():
                 project_back(j - 1, rows)
     raw_sum.collect()
     take(layers - 1)
@@ -647,7 +647,11 @@
             time_step * dot6(jnp.concatenate(slopes + [-item.T for item in slopes], axis=1), trans[...])
         )
 
-    back_last = [functools.partial(project_back, layers - 1, rows) for rows in quarters]
+    def finish_back(rows):
+        project_back(layers - 2, rows)
+        project_back(layers - 1, rows)
+
+    back_last = [functools.partial(finish_back, rows) for rows in quarters]
     fillers = [functools.partial(slope_product, d) for d in (0, 2, 1)] + [drive]
     fillers += [back_last[0], lambda: (raw_sum.share(), back_last[1]()), back_last[2]]
     fillers += [lambda: (raw_sum.finish(), back_last[3]())]
@@ -699,7 +703,7 @@
     g2[slab] = gx[core] + g1[...]
     mine = g2.at[slab]
     copies = [
-        send(mine, mine, ref["gss"].at[k - 1], ref["gsr"].at[k - 1], pos.slab_at(k)[1]) for k in range(1, slabs)
+        send(mine, mine, ref["gss"].at[k - 1], ref["gsr"].at[k - 1], (pos.slab_mate(k), brick)) for k in range(1, slabs)
     ]
     ref["basis_x"][...] = dot3(advanced, turned)
     sent = len(started) - len(copies)

time: 70.5 us -> 70.4 us (level)
  no operation moved by 1% of the time
where the time goes in v7:
time: 70.4 us; the launch traced here: 70.2 us
  Pallas kernels  69.4 us (99%)
  between operations  0.8 us (1%)
    pallas_call x1, Pallas kernels, local(): pl.pallas_call(functools.partial(step_kernel, tuple(names), slabs, layers...  63.7 us
    pallas_call x1, Pallas kernels, local(): pl.pallas_call(finish_kernel, out_shape=(jax.ShapeDtypeStruct((own, rank)...  5.76 us

profile of v7, /device:TPU:0, one launch (start us, length us, event | category | flops | bytes accessed | tf_op | source)
XLA Modules:
  0.0 70.2 jit_solution(63772738171757886)
XLA Ops:
  0.6 63.7 %shard_map.49 = (f32[64,128]{1,0:T(8,128)S(1)}, f32[128,128]{1,0:T(8,128)S(1)}, f32[1024,128]{1,0:T(8,128)S(1)}) custom-call(f32[2,2,16,128]{3,2,1,0:T(8,128)} %refs_0_.1, f32[1024,128]{1,0:T(8,128)} %refs_1_.1), custom_call_target="tpu_custom_call" | custom-call | tf_op jit(solution)/shard_map/pallas_call | solution.py:850
  64.3 5.8 %shard_map.50 = (f32[64,128]{1,0:T(8,128)}, f32[128,128]{1,0:T(8,128)}, f32[1024,128]{1,0:T(8,128)}) custom-call(f32[128,128]{1,0:T(8,128)S(1)} %get-tuple-element.9.gram, f32[1024,128]{1,0:T(8,128)S(1)} %get-tuple-element.10.lnew, f32[64,128]{1,0:T(8,128)S(1)} %get-tuple-element.11.field), custom_call_target="tpu_custom_call" | custom-call | tf_op jit(solution)/shard_map/pallas_call | solution.py:865
